TPU v7x, 32 devices: a whole 2x2x4 slice. The times are simulated.
32 devices in a mesh: dp: 8 (over z, x), tensor: 4 (over y, core).
Axes of the slice: x: 2, y: 2, z: 4, core: 2. Of those that a mesh axis runs over, the one named last changes fastest.
Arguments:
- inputs: bfloat16 [16, 1024, 1024], P('dp'), may hold values from -6 to 6
- segment_ids: int32 [16, 1024], P('dp'), may hold values from 0 to 7, never falling along the last dimension, each value on 1 to 512 neighbouring positions
- doc_offsets: int32 [16, 8], P('dp'), may hold values from 0 to 3071
- time_index: int32 [16], P('dp'), may hold values from 0 to 999
- w_qkv: bfloat16 [3, 1024, 1024], P(None, 'dp', 'tensor'), may hold values from -0.1875 to 0.1875
- w_out: bfloat16 [1024, 1024], P('tensor', 'dp'), may hold values from -0.75 to 0.75
- w_up: bfloat16 [1024, 4096], P('dp', 'tensor'), may hold values from -0.1875 to 0.1875
- w_down: bfloat16 [4096, 1024], P('tensor', 'dp'), may hold values from -0.09375 to 0.09375
- w_time: bfloat16 [256, 1024], P(None, 'dp'), may hold values from -0.375 to 0.375
- gain_attn: bfloat16 [1024], P('dp'), may hold values from 0.5 to 1.5
- gain_mlp: bfloat16 [1024], P('dp'), may hold values from 0.5 to 1.5
- cotangent: bfloat16 [16, 1024, 1024], P('dp'), may hold values from -6 to 6
Outputs:
- block_out: bfloat16 [16, 1024, 1024], P('dp', None, 'tensor')
- input_grad: float32 [16, 1024, 1024], P('dp', None, 'tensor')
- grad_qkv: float32 [3, 1024, 1024], P(None, 'dp', 'tensor')
- grad_out: float32 [1024, 1024], P('tensor', 'dp')
- grad_up: float32 [1024, 4096], P('dp', 'tensor')
- grad_down: float32 [4096, 1024], P('tensor', 'dp')
- grad_time: float32 [256, 1024], P(None, 'dp')
- grad_gain_attn: float32 [1024], P('dp')
- grad_gain_mlp: float32 [1024], P('dp')
Inputs may be any that keep to these rules, and one draw needn't show every extreme that they name: `segment_ids`: in each sequence the ids never fall, every id of 0 to 7 occurs, each document has 1 to 512 tokens and one has exactly 512.
All inputs are finite; a program needn't handle non-finite values.
Results may differ from a plain program's by a relative error of at most 0.022.
Values may be sent and summed in bfloat16 or wider, within the bound.
No kernel may reach another device: no remote copies, remote signals or barrier semaphores. Data moves between devices by JAX's collectives and lax.ppermute only.
A program may use at most 192 MiB of HBM per device.

v0:
```python
import math

import jax
import jax.numpy as jnp
from jax import lax
from jax.sharding import PartitionSpec as P

HEADS = 16
TEMB = 256


eps = 1e-05
masked = -1000000000.0


def sinusoid(values, width):
    half = width // 2
    freqs = jnp.exp(-math.log(10000.0) * jnp.arange(half, dtype=jnp.float32) / half)
    angles = values[..., None] * freqs
    return jnp.concatenate([jnp.sin(angles), jnp.cos(angles)], axis=-1)


def layer_norm(hidden, gain):
    centre = jnp.mean(hidden, axis=-1, keepdims=True)
    centred = hidden - centre
    spread = jnp.mean(centred * centred, axis=-1, keepdims=True)
    return centred * lax.rsqrt(spread + eps) * gain


def positions(segs, offsets):
    seq_len = segs.shape[0]
    index = jnp.arange(seq_len, dtype=jnp.int32)
    member = segs[:, None] == jnp.arange(offsets.shape[0], dtype=jnp.int32)[None, :]
    starts = jnp.min(jnp.where(member, index[:, None], seq_len), axis=0)
    start_tok = jnp.sum(jnp.where(member, starts[None, :], 0), axis=1)
    offset_tok = jnp.sum(jnp.where(member, offsets[None, :], 0), axis=1)
    return offset_tok + index - start_tok


def attend(query, key, value, same, scale):
    seq_len = query.shape[0]
    rows = min(512, seq_len)
    outputs = []
    totals = []
    for first in range(0, seq_len, rows):
        q_part = query[first : first + rows]
        scores = jnp.einsum("qhe,khe->hqk", q_part, key, preferred_element_type=jnp.float32) * scale
        scores = jnp.where(same[None, first : first + rows], scores, masked)
        top = jnp.max(scores, axis=-1, keepdims=True)
        expo = jnp.exp(scores - top)
        denom = jnp.sum(expo, axis=-1, keepdims=True)
        probs = (expo / denom).astype(jnp.bfloat16)
        outputs.append(jnp.einsum("hqk,khe->qhe", probs, value, preferred_element_type=jnp.float32))
        totals.append(top + jnp.log(denom))
    return (jnp.concatenate(outputs, axis=0), jnp.concatenate(totals, axis=1))


def attend_back(query, key, value, same, scale, lse, d_mixed):
    seq_len = query.shape[0]
    rows = min(512, seq_len)
    d_key = jnp.zeros(key.shape, jnp.float32)
    d_value = jnp.zeros(value.shape, jnp.float32)
    d_query = []
    for first in range(0, seq_len, rows):
        q_part = query[first : first + rows]
        g_part = d_mixed[first : first + rows]
        scores = jnp.einsum("qhe,khe->hqk", q_part, key, preferred_element_type=jnp.float32) * scale
        scores = jnp.where(same[None, first : first + rows], scores, masked)
        probs = jnp.exp(scores - lse[:, first : first + rows])
        d_probs = jnp.einsum("qhe,khe->hqk", g_part, value, preferred_element_type=jnp.float32)
        d_value = d_value + jnp.einsum(
            "hqk,qhe->khe", probs.astype(jnp.bfloat16), g_part, preferred_element_type=jnp.float32
        )
        delta = jnp.sum(probs * d_probs, axis=-1, keepdims=True)
        d_scores = (probs * (d_probs - delta)).astype(jnp.bfloat16)
        d_query.append(
            jnp.einsum("hqk,khe->qhe", d_scores, key, preferred_element_type=jnp.float32) * scale
        )
        d_key = (
            d_key
            + jnp.einsum("hqk,qhe->khe", d_scores, q_part, preferred_element_type=jnp.float32)
            * scale
        )
    return (jnp.concatenate(d_query, axis=0), d_key, d_value)


def shards(
    inputs,
    segment_ids,
    doc_offsets,
    time_index,
    w_qkv,
    w_out,
    w_up,
    w_down,
    w_time,
    gain_attn,
    gain_mlp,
    cotangent,
):
    n_dp = lax.axis_size("dp")
    n_tensor = lax.axis_size("tensor")
    member_index = lax.axis_index("tensor")
    seqs_dev, seq_len, width = inputs.shape
    shard = width // n_tensor
    head_size = width // HEADS
    heads_dev = shard // head_size
    scale = head_size ** (-0.5)
    hidden_dev = w_up.shape[1]

    def step(carry, items):
        x_seq, segs, offsets, time_now, cot = items
        fwd_w = (
            lax.all_gather(w_qkv, "dp", axis=1, tiled=True),
            lax.all_gather(w_out, "dp", axis=1, tiled=True),
            lax.all_gather(w_up, "dp", axis=0, tiled=True),
            lax.all_gather(w_down, "dp", axis=1, tiled=True),
            lax.all_gather(w_time, "dp", axis=1, tiled=True),
            lax.all_gather(gain_attn, "dp", axis=0, tiled=True),
            lax.all_gather(gain_mlp, "dp", axis=0, tiled=True),
        )
        qkv_w, out_w, up_w, down_w, time_w, attn_g, mlp_g = fwd_w
        embed = sinusoid(positions(segs, offsets).astype(jnp.float32), width)
        temb = sinusoid(time_now.astype(jnp.float32), TEMB)
        same = segs[:, None] == segs[None, :]
        cond = jnp.dot(temb, time_w.astype(jnp.float32), precision=lax.Precision.HIGHEST)
        h0 = x_seq.astype(jnp.float32) + embed + cond[None, :]
        n1 = layer_norm(h0, attn_g.astype(jnp.float32)).astype(jnp.bfloat16)
        qkv = jnp.einsum("sd,cde->cse", n1, qkv_w, preferred_element_type=jnp.float32).astype(
            jnp.bfloat16
        )
        query = qkv[0].reshape(seq_len, heads_dev, head_size)
        key = qkv[1].reshape(seq_len, heads_dev, head_size)
        value = qkv[2].reshape(seq_len, heads_dev, head_size)
        mixed, lse = attend(query, key, value, same, scale)
        mixed = mixed.reshape(seq_len, shard).astype(jnp.bfloat16)
        attn_term = jnp.dot(mixed, out_w, preferred_element_type=jnp.float32)
        h1 = h0 + lax.psum(attn_term.astype(jnp.bfloat16), "tensor").astype(jnp.float32)
        n2 = layer_norm(h1, mlp_g.astype(jnp.float32)).astype(jnp.bfloat16)
        hidden = jnp.dot(n2, up_w, preferred_element_type=jnp.float32)
        active = jax.nn.gelu(hidden, approximate=False).astype(jnp.bfloat16)
        down_term = jnp.dot(active, down_w, preferred_element_type=jnp.float32)
        down_share = lax.psum_scatter(
            down_term.astype(jnp.bfloat16), "tensor", scatter_dimension=1, tiled=True
        ).astype(jnp.float32)
        h1_share = lax.dynamic_slice_in_dim(h1, member_index * shard, shard, 1)
        out_share = (h1_share + down_share).astype(jnp.bfloat16)
        bwd_w = (
            lax.all_gather(w_qkv, "dp", axis=1, tiled=True),
            lax.all_gather(w_out, "dp", axis=1, tiled=True),
            lax.all_gather(w_up, "dp", axis=0, tiled=True),
            lax.all_gather(w_down, "dp", axis=1, tiled=True),
            lax.all_gather(w_time, "dp", axis=1, tiled=True),
            lax.all_gather(gain_attn, "dp", axis=0, tiled=True),
            lax.all_gather(gain_mlp, "dp", axis=0, tiled=True),
        )
        qkv_w, out_w, up_w, down_w, time_w, attn_g, mlp_g = bwd_w
        d_active = jnp.einsum("sd,fd->sf", cot, down_w, preferred_element_type=jnp.float32)
        gelu_value, gelu_back = jax.vjp(lambda arg: jax.nn.gelu(arg, approximate=False), hidden)
        d_hidden = gelu_back(d_active)[0].astype(jnp.bfloat16)
        grad_down = jnp.einsum("sf,sd->fd", active, cot, preferred_element_type=jnp.float32)
        grad_up = jnp.einsum("sd,sf->df", n2, d_hidden, preferred_element_type=jnp.float32)
        d_n2_term = jnp.einsum("sf,df->sd", d_hidden, up_w, preferred_element_type=jnp.float32)
        d_n2 = lax.psum(d_n2_term.astype(jnp.bfloat16), "tensor").astype(jnp.float32)
        norm_value, norm_back = jax.vjp(layer_norm, h1, mlp_g.astype(jnp.float32))
        d_h1_norm, grad_mlp_gain = norm_back(d_n2)
        d_h1 = cot.astype(jnp.float32) + d_h1_norm
        d_h1_low = d_h1.astype(jnp.bfloat16)
        grad_out = jnp.einsum("sa,sd->ad", mixed, d_h1_low, preferred_element_type=jnp.float32)
        d_mixed = jnp.einsum(
            "sd,ad->sa", d_h1_low, out_w, preferred_element_type=jnp.float32
        ).astype(jnp.bfloat16)
        d_query, d_key, d_value = attend_back(
            query, key, value, same, scale, lse, d_mixed.reshape(seq_len, heads_dev, head_size)
        )
        d_qkv = jnp.stack(
            [
                d_query.reshape(seq_len, shard),
                d_key.reshape(seq_len, shard),
                d_value.reshape(seq_len, shard),
            ],
            axis=0,
        ).astype(jnp.bfloat16)
        grad_qkv = jnp.einsum("sd,cse->cde", n1, d_qkv, preferred_element_type=jnp.float32)
        d_n1_term = jnp.einsum("cse,cde->sd", d_qkv, qkv_w, preferred_element_type=jnp.float32)
        d_n1 = lax.psum(d_n1_term.astype(jnp.bfloat16), "tensor").astype(jnp.float32)
        first_value, first_back = jax.vjp(layer_norm, h0, attn_g.astype(jnp.float32))
        d_h0_norm, grad_attn_gain = first_back(d_n1)
        d_h0 = d_h1 + d_h0_norm
        grad_time = temb[:, None] * jnp.sum(d_h0, axis=0)[None, :]
        grad_share = lax.dynamic_slice_in_dim(d_h0, member_index * shard, shard, 1)
        grads = (grad_qkv, grad_out, grad_up, grad_down, grad_time, grad_attn_gain, grad_mlp_gain)
        carry = tuple((total + part for total, part in zip(carry, grads)))
        return (carry, (out_share, grad_share))

    start = (
        jnp.zeros((3, width, shard), jnp.float32),
        jnp.zeros((shard, width), jnp.float32),
        jnp.zeros((width, hidden_dev), jnp.float32),
        jnp.zeros((hidden_dev, width), jnp.float32),
        jnp.zeros((w_time.shape[0], width), jnp.float32),
        jnp.zeros((width,), jnp.float32),
        jnp.zeros((width,), jnp.float32),
    )
    carry, (block_out, input_grad) = lax.scan(
        step, start, (inputs, segment_ids, doc_offsets, time_index, cotangent)
    )
    shares = (
        lax.psum_scatter(
            carry[0].astype(jnp.bfloat16), "dp", scatter_dimension=1, tiled=True
        ).astype(jnp.float32),
        lax.psum_scatter(
            carry[1].astype(jnp.bfloat16), "dp", scatter_dimension=1, tiled=True
        ).astype(jnp.float32),
        lax.psum_scatter(
            carry[2].astype(jnp.bfloat16), "dp", scatter_dimension=0, tiled=True
        ).astype(jnp.float32),
        lax.psum_scatter(
            carry[3].astype(jnp.bfloat16), "dp", scatter_dimension=1, tiled=True
        ).astype(jnp.float32),
        lax.psum_scatter(
            carry[4].astype(jnp.bfloat16), "dp", scatter_dimension=1, tiled=True
        ).astype(jnp.float32),
        lax.psum_scatter(
            carry[5].astype(jnp.bfloat16), "dp", scatter_dimension=0, tiled=True
        ).astype(jnp.float32),
        lax.psum_scatter(
            carry[6].astype(jnp.bfloat16), "dp", scatter_dimension=0, tiled=True
        ).astype(jnp.float32),
    )
    factor = float(n_dp * seqs_dev * seq_len) ** (-0.5)
    return (
        block_out,
        input_grad,
        shares[0] * factor,
        shares[1] * factor,
        shares[2] * factor,
        shares[3] * factor,
        shares[4] * factor,
        shares[5] * factor,
        shares[6] * factor,
    )


def solution(mesh):
    in_specs = (
        P("dp", None, None),
        P("dp", None),
        P("dp", None),
        P("dp"),
        P(None, "dp", "tensor"),
        P("tensor", "dp"),
        P("dp", "tensor"),
        P("tensor", "dp"),
        P(None, "dp"),
        P("dp"),
        P("dp"),
        P("dp", None, None),
    )
    out_specs = (
        P("dp", None, "tensor"),
        P("dp", None, "tensor"),
        P(None, "dp", "tensor"),
        P("tensor", "dp"),
        P("dp", "tensor"),
        P("tensor", "dp"),
        P(None, "dp"),
        P("dp"),
        P("dp"),
    )
    return jax.shard_map(shards, mesh=mesh, in_specs=in_specs, out_specs=out_specs, check_vma=False)
```

profile of v0, /device:TPU:0, one launch (start us, length us, event | category | flops | bytes accessed | tf_op | source)
XLA Modules:
  0.0 1271.8 jit_solution(9594301734309655532)
XLA Ops:
  9.2 912.2 %while.29 = (s32[]{:T(128)}, f32[3,1024,256]{1,2,0:T(8,128)}, f32[256,1024]{1,0:T(8,128)}, f32[1024,1024]{1,0:T(8,128)}, f32[1024,1024]{1,0:T(8,128)}, /*index=5...) while((s32[]{:T(128)}, f32[3,1024,256]{1,2,0:T(8,128)}, ...), condition=%wide.region_25.26_spmd.clone, body=%wide.region_0.25_spmd.clone.sunk | while | flops 22813945856 | bytes 895582016 | solution.py:205
  14.1 22.4 %all-gather.6 = bf16[8,1,128]{2,1,0:T(2,128)(2,1)S(1)} all-gather(bf16[1,1,128]{2,1,0:T(2,128)(2,1)} %bitcast.299), channel_id=1, replica_groups=mesh['dp'=8,'tensor'=4] {'dp'}, dimensions={0}, use_global_device_ids=true | all-gather | bytes 2304 | tf_op jit(solution)/shard_map/while/body/eval_jaxpr/all_gather | solution.py:119
  36.5 30.0 %all_gather.59 = bf16[256,1024]{1,0:T(8,128)(2,1)S(1)} all-gather(bf16[256,128]{1,0:T(8,128)(2,1)} %get-tuple-element.818), channel_id=1, replica_groups=mesh['dp'=8,'tensor'=4] {'dp'}, dimensions={1}, use_global_device_ids=true | all-gather | bytes 589824 | tf_op jit(solution)/shard_map/while/body/eval_jaxpr/all_gather | solution.py:118
  66.8 7.3 multiply_sine_fusion.2
  77.4 27.4 %all_gather.61 = bf16[256,1024]{1,0:T(8,128)(2,1)S(1)} all-gather(bf16[256,128]{1,0:T(8,128)(2,1)S(1)} %copy-done.35), channel_id=1, replica_groups=mesh['dp'=8,'tensor'=4] {'dp'}, dimensions={1}, use_global_device_ids=true | all-gather | bytes 589824 | tf_op jit(solution)/shard_map/while/body/eval_jaxpr/all_gather | solution.py:115
  105.5 4.7 fusion.249
  129.1 17.2 %all-gather.7 = bf16[8,1,128]{2,1,0:T(2,128)(2,1)S(1)} all-gather(bf16[1,1,128]{2,1,0:T(2,128)(2,1)S(1)} %bitcast.300), channel_id=1, replica_groups=mesh['dp'=8,'tensor'=4] {'dp'}, dimensions={0}, use_global_device_ids=true | all-gather | bytes 2304 | tf_op jit(solution)/shard_map/while/body/eval_jaxpr/all_gather | solution.py:120
  146.3 30.1 %all-reduce.7.cloned.1.call-done = bf16[1024,1024]{1,0:T(8,128)(2,1)} async-done(((bf16[1024,1024]{1,0:T(8,128)(2,1)}), bf16[1024,1024]{1,0:T(8,128)(2,1)}) %all-reduce.7.cloned.1.call-update) | async-done | bytes 2097168 | tf_op jit(solution)/shard_map/while/body/eval_jaxpr/psum | solution.py:138
  176.4 3.3 fusion.259
  182.4 45.6 %all-gather.12.cloned.1.call-done = bf16[1024,1024]{1,0:T(8,128)(2,1)} async-done(((bf16[128,1024]{1,0:T(8,128)(2,1)}), bf16[1024,1024]{1,0:T(8,128)(2,1)}) %all-gather.12.cloned.1.call-update) | async-done | bytes 2097168 | tf_op jit(solution)/shard_map/while/body/eval_jaxpr/all_gather | solution.py:116
  228.0 15.4 %multiply_convert_fusion.12 = (bf16[1024,1024]{1,0:T(8,128)(2,1)}, f32[1024,1024]{1,0:T(8,128)}, f32[1024,1024]{1,0:T(8,128)}) fusion(bf16[1024,1024]{1,0:T(8,128)(2,1)} %all-gather.12.cloned.1.call-done, f32[1024,1024]{1,0:T(8,128)} %copy-done.5, f32[1024]{0:T(1024)S(1)} %bitcast.290, f32[1024]{0:T(1024)S(1)} %fusion.260, ...), kind=kOutput, calls=%fused_computation.40.clone.1 | convolution fusion | flops 2219835392 | bytes 16789504 | tf_op jit(solution)/shard_map/while/body/eval_jaxpr/dot_general | solution.py:140
  243.4 36.0 %all-gather.16.cloned.1.call-done = bf16[1024,1024]{1,0:T(8,128)(2,1)} async-done(((bf16[1024,128]{1,0:T(8,128)(2,1)}), bf16[1024,1024]{1,0:T(8,128)(2,1)}) %all-gather.16.cloned.1.call-update) | async-done | bytes 2097168 | tf_op jit(solution)/shard_map/while/body/eval_jaxpr/all_gather | solution.py:152
  279.4 8.2 add_convert_fusion.3
  288.9 3.8 convolution_convert_fusion.10
  292.9 49.5 %all-reduce.9.cloned.1.call-done = bf16[1024,1024]{1,0:T(8,128)(2,1)} async-done(((bf16[1024,1024]{1,0:T(8,128)(2,1)}), bf16[1024,1024]{1,0:T(8,128)(2,1)}) %all-reduce.9.cloned.1.call-update) | async-done | bytes 2097168 | tf_op jit(solution)/shard_map/while/body/eval_jaxpr/psum | solution.py:164
  342.4 4.4 fusion.261
  354.9 2.6 multiply_reduce_fusion.10
  364.9 2.6 multiply_reduce_fusion.11
  373.9 3.2 bitcast_convert_fusion.2
  377.4 5.9 convolution_convert_fusion.12
  383.3 7.6 select_add_fusion.10
  391.0 3.0 select_add_fusion.11
  398.1 3.6 bitcast_add_fusion.2
  401.7 27.0 %all-reduce.11.cloned.1.call-done = bf16[1024,1024]{1,0:T(8,128)(2,1)} async-done(((bf16[1024,1024]{1,0:T(8,128)(2,1)}), bf16[1024,1024]{1,0:T(8,128)(2,1)}) %all-reduce.11.cloned.1.call-update) | async-done | bytes 2097168 | tf_op jit(solution)/shard_map/while/body/eval_jaxpr/psum | solution.py:186
  428.7 3.8 fusion.271
  433.4 2.7 fusion.272
  436.2 3.9 fusion.273
  441.8 20.9 %reduce-scatter.23.cloned.1.call-done = bf16[1024,256]{1,0:T(8,128)(2,1)} async-done(((bf16[1024,1024]{1,0:T(8,128)(2,1)}), bf16[1024,256]{1,0:T(8,128)(2,1)}) %reduce-scatter.23.cloned.1.call-update) | async-done | bytes 524304 | tf_op jit(solution)/shard_map/while/body/eval_jaxpr/reduce_scatter | solution.py:143
  470.3 20.7 %all-gather.6 = bf16[8,1,128]{2,1,0:T(2,128)(2,1)S(1)} all-gather(bf16[1,1,128]{2,1,0:T(2,128)(2,1)} %bitcast.299), channel_id=1, replica_groups=mesh['dp'=8,'tensor'=4] {'dp'}, dimensions={0}, use_global_device_ids=true | all-gather | bytes 2304 | tf_op jit(solution)/shard_map/while/body/eval_jaxpr/all_gather | solution.py:119
  491.0 29.8 %all_gather.59 = bf16[256,1024]{1,0:T(8,128)(2,1)S(1)} all-gather(bf16[256,128]{1,0:T(8,128)(2,1)} %get-tuple-element.818), channel_id=1, replica_groups=mesh['dp'=8,'tensor'=4] {'dp'}, dimensions={1}, use_global_device_ids=true | all-gather | bytes 589824 | tf_op jit(solution)/shard_map/while/body/eval_jaxpr/all_gather | solution.py:118
  521.1 7.3 multiply_sine_fusion.2
  531.7 27.2 %all_gather.61 = bf16[256,1024]{1,0:T(8,128)(2,1)S(1)} all-gather(bf16[256,128]{1,0:T(8,128)(2,1)S(1)} %copy-done.35), channel_id=1, replica_groups=mesh['dp'=8,'tensor'=4] {'dp'}, dimensions={1}, use_global_device_ids=true | all-gather | bytes 589824 | tf_op jit(solution)/shard_map/while/body/eval_jaxpr/all_gather | solution.py:115
  559.7 4.7 fusion.249
  583.3 17.0 %all-gather.7 = bf16[8,1,128]{2,1,0:T(2,128)(2,1)S(1)} all-gather(bf16[1,1,128]{2,1,0:T(2,128)(2,1)S(1)} %bitcast.300), channel_id=1, replica_groups=mesh['dp'=8,'tensor'=4] {'dp'}, dimensions={0}, use_global_device_ids=true | all-gather | bytes 2304 | tf_op jit(solution)/shard_map/while/body/eval_jaxpr/all_gather | solution.py:120
  600.3 29.5 %all-reduce.7.cloned.1.call-done = bf16[1024,1024]{1,0:T(8,128)(2,1)} async-done(((bf16[1024,1024]{1,0:T(8,128)(2,1)}), bf16[1024,1024]{1,0:T(8,128)(2,1)}) %all-reduce.7.cloned.1.call-update) | async-done | bytes 2097168 | tf_op jit(solution)/shard_map/while/body/eval_jaxpr/psum | solution.py:138
  629.8 3.3 fusion.259
  635.8 45.4 %all-gather.12.cloned.1.call-done = bf16[1024,1024]{1,0:T(8,128)(2,1)} async-done(((bf16[128,1024]{1,0:T(8,128)(2,1)}), bf16[1024,1024]{1,0:T(8,128)(2,1)}) %all-gather.12.cloned.1.call-update) | async-done | bytes 2097168 | tf_op jit(solution)/shard_map/while/body/eval_jaxpr/all_gather | solution.py:116
  681.2 15.4 %multiply_convert_fusion.12 = (bf16[1024,1024]{1,0:T(8,128)(2,1)}, f32[1024,1024]{1,0:T(8,128)}, f32[1024,1024]{1,0:T(8,128)}) fusion(bf16[1024,1024]{1,0:T(8,128)(2,1)} %all-gather.12.cloned.1.call-done, f32[1024,1024]{1,0:T(8,128)} %copy-done.5, f32[1024]{0:T(1024)S(1)} %bitcast.290, f32[1024]{0:T(1024)S(1)} %fusion.260, ...), kind=kOutput, calls=%fused_computation.40.clone.1 | convolution fusion | flops 2219835392 | bytes 16789504 | tf_op jit(solution)/shard_map/while/body/eval_jaxpr/dot_general | solution.py:140
  696.6 36.2 %all-gather.16.cloned.1.call-done = bf16[1024,1024]{1,0:T(8,128)(2,1)} async-done(((bf16[1024,128]{1,0:T(8,128)(2,1)}), bf16[1024,1024]{1,0:T(8,128)(2,1)}) %all-gather.16.cloned.1.call-update) | async-done | bytes 2097168 | tf_op jit(solution)/shard_map/while/body/eval_jaxpr/all_gather | solution.py:152
  732.8 8.2 add_convert_fusion.3
  742.3 3.8 convolution_convert_fusion.10
  746.6 49.2 %all-reduce.9.cloned.1.call-done = bf16[1024,1024]{1,0:T(8,128)(2,1)} async-done(((bf16[1024,1024]{1,0:T(8,128)(2,1)}), bf16[1024,1024]{1,0:T(8,128)(2,1)}) %all-reduce.9.cloned.1.call-update) | async-done | bytes 2097168 | tf_op jit(solution)/shard_map/while/body/eval_jaxpr/psum | solution.py:164
  795.9 4.4 fusion.261
  808.3 2.6 multiply_reduce_fusion.10
  818.3 2.6 multiply_reduce_fusion.11
  827.3 3.2 bitcast_convert_fusion.2
  830.8 5.9 convolution_convert_fusion.12
  836.7 8.8 select_add_fusion.10
  845.6 3.0 select_add_fusion.11
  852.7 5.5 bitcast_add_fusion.2
  858.2 23.9 %all-reduce.11.cloned.1.call-done = bf16[1024,1024]{1,0:T(8,128)(2,1)} async-done(((bf16[1024,1024]{1,0:T(8,128)(2,1)}), bf16[1024,1024]{1,0:T(8,128)(2,1)}) %all-reduce.11.cloned.1.call-update) | async-done | bytes 2097168 | tf_op jit(solution)/shard_map/while/body/eval_jaxpr/psum | solution.py:186
  882.1 3.8 fusion.271
  886.8 2.7 fusion.272
  889.6 3.9 fusion.273
  895.2 20.8 %reduce-scatter.23.cloned.1.call-done = bf16[1024,256]{1,0:T(8,128)(2,1)} async-done(((bf16[1024,1024]{1,0:T(8,128)(2,1)}), bf16[1024,256]{1,0:T(8,128)(2,1)}) %reduce-scatter.23.cloned.1.call-update) | async-done | bytes 524304 | tf_op jit(solution)/shard_map/while/body/eval_jaxpr/reduce_scatter | solution.py:143
  926.3 3.1 copy.32
  931.9 2.6 copy.37
  934.6 3.9 convert_element_type.241
  939.8 21.4 %all-reduce.2 = (bf16[1024]{0:T(1024)(128)(2,1)S(1)}, bf16[1024]{0:T(1024)(128)(2,1)S(1)}) all-reduce(bf16[1024]{0:T(1024)(128)(2,1)S(1)} %convert_element_type.247, bf16[1024]{0:T(1024)(128)(2,1)S(1)} %convert_element_type.249), channel_id=8, replica_groups=mesh['dp'=8,'tensor'=4] {'dp'}, use_global_device_ids=true, to_apply=%region_31.32.clone | all-reduce | flops 2048 | bytes 8192
  961.8 26.1 %reduce-scatter.17.cloned.1.call-done = bf16[128,256]{1,0:T(8,128)(2,1)} async-done(((bf16[1024,256]{1,0:T(8,128)(2,1)}), bf16[128,256]{1,0:T(8,128)(2,1)}) %reduce-scatter.17.cloned.1.call-update) | async-done | bytes 65552
  988.9 64.2 %reduce-scatter.21.cloned.1.call-done = bf16[128,256]{1,0:T(8,128)(2,1)} async-done(((bf16[1024,256]{1,0:T(8,128)(2,1)}), bf16[128,256]{1,0:T(8,128)(2,1)}) %reduce-scatter.21.cloned.1.call-update) | async-done | bytes 65552
  1055.4 65.6 %reduce-scatter.13.cloned.1.call-done = bf16[3,128,256]{2,1,0:T(8,128)(2,1)} async-done(((bf16[3,1024,256]{2,1,0:T(8,128)(2,1)}), bf16[3,128,256]{2,1,0:T(8,128)(2,1)}) %reduce-scatter.13.cloned.1.call-update) | async-done | bytes 196624 | tf_op jit(solution)/shard_map/reduce_scatter | solution.py:209
  1122.7 69.0 %reduce-scatter.19.cloned.1.call-done = bf16[128,1024]{1,0:T(8,128)(2,1)} async-done(((bf16[1024,1024]{1,0:T(8,128)(2,1)}), bf16[128,1024]{1,0:T(8,128)(2,1)}) %reduce-scatter.19.cloned.1.call-update) | async-done | bytes 262160
  1193.7 68.7 %reduce-scatter.15.cloned.1.call-done = bf16[128,1024]{1,0:T(8,128)(2,1)} async-done(((bf16[1024,1024]{1,0:T(8,128)(2,1)}), bf16[128,1024]{1,0:T(8,128)(2,1)}) %reduce-scatter.15.cloned.1.call-update) | async-done | bytes 262160 | tf_op jit(solution)/shard_map/reduce_scatter | solution.py:215
  (417 shorter events, 142.5 us)
Async XLA Ops:
  9.5 96.0 %all-gather.14.cloned.1.call-start = ((), (), s32[]{:S(2)}) async-start(), calls=%async_computation.12 | async-start | bytes 1769472 | tf_op jit(solution)/shard_map/while/body/eval_jaxpr/all_gather | solution.py:114
  10.2 166.2 %all-reduce.7.cloned.1.call-start = ((), (), s32[]{:S(2)}) async-start(), calls=%async_computation.13 | async-start | bytes 4194304 | tf_op jit(solution)/shard_map/while/body/eval_jaxpr/psum | solution.py:138
  10.3 63.9 %copy-start.30 = (bf16[2,1024,1024]{2,1,0:T(8,128)(2,1)S(1)}, bf16[2,1024,1024]{2,1,0:T(8,128)(2,1)}, u32[]{:S(2)}) copy-start(bf16[2,1024,1024]{2,1,0:T(8,128)(2,1)} %get-tuple-element.814) | copy-start | bytes 12582916 | tf_op jit(solution)/shard_map/while
  14.1 60.8 %copy-start.38 = (f32[256]{0:T(256)}, f32[256]{0:T(256)S(1)}, u32[]{:S(2)}) copy-start(f32[256]{0:T(256)S(1)} %pad_maximum_fusion.13) | copy-start | bytes 3076 | tf_op jit(solution)/shard_map/while
  77.4 32.8 %copy-start.36 = (f32[1024]{0:T(1024)}, f32[1024]{0:T(1024)S(1)}, u32[]{:S(2)}) copy-start(f32[1024]{0:T(1024)S(1)} %multiply_reduce_fusion.8) | copy-start | bytes 12292 | tf_op jit(solution)/shard_map/while
  110.3 7.3 copy-start.18
  127.7 100.2 %all-gather.12.cloned.1.call-start = ((), (), s32[]{:S(2)}) async-start(), calls=%async_computation.11 | async-start | bytes 2359296 | tf_op jit(solution)/shard_map/while/body/eval_jaxpr/all_gather | solution.py:116
  128.5 150.9 %all-gather.16.cloned.1.call-start = ((), (), s32[]{:S(2)}) async-start(), calls=%async_computation.14 | async-start | bytes 2359296 | tf_op jit(solution)/shard_map/while/body/eval_jaxpr/all_gather | solution.py:152
  129.1 213.4 %all-reduce.9.cloned.1.call-start = ((), (), s32[]{:S(2)}) async-start(), calls=%async_computation.15 | async-start | bytes 4194304 | tf_op jit(solution)/shard_map/while/body/eval_jaxpr/psum | solution.py:164
  279.4 9.5 copy-start.47
  292.7 136.0 %all-reduce.11.cloned.1.call-start = ((), (), s32[]{:S(2)}) async-start(), calls=%async_computation.16 | async-start | bytes 4194304 | tf_op jit(solution)/shard_map/while/body/eval_jaxpr/psum | solution.py:186
  342.4 4.7 copy-start.11
  349.3 5.5 slice-start.1
  351.1 6.3 copy-start.12
  352.6 4.8 copy-start.22
  357.4 5.7 slice-start.2
  357.4 5.7 slice-start.3
  377.1 85.6 %reduce-scatter.23.cloned.1.call-start = ((), (), s32[]{:S(2)}) async-start(), calls=%async_computation.17 | async-start | bytes 2621440 | tf_op jit(solution)/shard_map/while/body/eval_jaxpr/reduce_scatter | solution.py:143
  383.3 7.6 copy-start.17
  383.3 7.6 copy-start.33
  383.3 7.6 copy-start.54
  394.0 7.6 copy-start.41
  396.1 5.5 copy-start.26
  401.7 30.9 %copy-start.37 = (f32[1024]{0:T(1024)S(1)}, f32[1024]{0:T(1024)}, u32[]{:S(2)}) copy-start(f32[1024]{0:T(1024)} %copy-done.36) | copy-start | bytes 12292 | tf_op jit(solution)/shard_map/while
  436.2 5.5 copy-start.27
  436.2 5.4 copy-start.39
  440.1 22.6 %copy-start.51 = (bf16[2,1024,256]{2,1,0:T(8,128)(2,1)S(1)}, bf16[2,1024,256]{2,1,0:T(8,128)(2,1)}, u32[]{:S(2)}) copy-start(bf16[2,1024,256]{2,1,0:T(8,128)(2,1)} %get-tuple-element.787) | copy-start | bytes 3145732 | tf_op jit(solution)/shard_map/while
  440.2 25.1 %copy-start.32 = (bf16[3,128,256]{1,2,0:T(8,128)(2,1)S(1)}, bf16[3,128,256]{1,2,0:T(8,128)(2,1)}, u32[]{:S(2)}) copy-start(bf16[3,128,256]{1,2,0:T(8,128)(2,1)} %copy-done.31) | copy-start | bytes 589828 | tf_op jit(solution)/shard_map/while
  440.3 23.9 %copy-start.44 = (f32[1024]{0:T(1024)}, f32[1024]{0:T(1024)S(1)}, u32[]{:S(2)}) copy-start(f32[1024]{0:T(1024)S(1)} %select_add_fusion.13) | copy-start | bytes 12292 | tf_op jit(solution)/shard_map/while
  441.8 22.5 %copy-start.28 = (f32[256,1024]{1,0:T(8,128)}, f32[256,1024]{1,0:T(8,128)S(1)}, u32[]{:S(2)}) copy-start(f32[256,1024]{1,0:T(8,128)S(1)} %select_add_fusion.12) | copy-start | bytes 3145732 | tf_op jit(solution)/shard_map/while
  465.7 94.0 %all-gather.14.cloned.1.call-start = ((), (), s32[]{:S(2)}) async-start(), calls=%async_computation.12 | async-start | bytes 1769472 | tf_op jit(solution)/shard_map/while/body/eval_jaxpr/all_gather | solution.py:114
  466.4 163.4 %all-reduce.7.cloned.1.call-start = ((), (), s32[]{:S(2)}) async-start(), calls=%async_computation.13 | async-start | bytes 4194304 | tf_op jit(solution)/shard_map/while/body/eval_jaxpr/psum | solution.py:138
  466.5 62.0 %copy-start.30 = (bf16[2,1024,1024]{2,1,0:T(8,128)(2,1)S(1)}, bf16[2,1024,1024]{2,1,0:T(8,128)(2,1)}, u32[]{:S(2)}) copy-start(bf16[2,1024,1024]{2,1,0:T(8,128)(2,1)} %get-tuple-element.814) | copy-start | bytes 12582916 | tf_op jit(solution)/shard_map/while
  470.3 58.9 %copy-start.38 = (f32[256]{0:T(256)}, f32[256]{0:T(256)S(1)}, u32[]{:S(2)}) copy-start(f32[256]{0:T(256)S(1)} %pad_maximum_fusion.13) | copy-start | bytes 3076 | tf_op jit(solution)/shard_map/while
  531.6 32.7 %copy-start.36 = (f32[1024]{0:T(1024)}, f32[1024]{0:T(1024)S(1)}, u32[]{:S(2)}) copy-start(f32[1024]{0:T(1024)S(1)} %multiply_reduce_fusion.8) | copy-start | bytes 12292 | tf_op jit(solution)/shard_map/while
  564.4 7.3 copy-start.18
  581.9 99.3 %all-gather.12.cloned.1.call-start = ((), (), s32[]{:S(2)}) async-start(), calls=%async_computation.11 | async-start | bytes 2359296 | tf_op jit(solution)/shard_map/while/body/eval_jaxpr/all_gather | solution.py:116
  582.5 150.4 %all-gather.16.cloned.1.call-start = ((), (), s32[]{:S(2)}) async-start(), calls=%async_computation.14 | async-start | bytes 2359296 | tf_op jit(solution)/shard_map/while/body/eval_jaxpr/all_gather | solution.py:152
  583.2 212.7 %all-reduce.9.cloned.1.call-start = ((), (), s32[]{:S(2)}) async-start(), calls=%async_computation.15 | async-start | bytes 4194304 | tf_op jit(solution)/shard_map/while/body/eval_jaxpr/psum | solution.py:164
  732.8 9.5 copy-start.47
  746.1 136.0 %all-reduce.11.cloned.1.call-start = ((), (), s32[]{:S(2)}) async-start(), calls=%async_computation.16 | async-start | bytes 4194304 | tf_op jit(solution)/shard_map/while/body/eval_jaxpr/psum | solution.py:186
  802.8 5.5 slice-start.1
  804.6 6.3 copy-start.12
  806.1 4.8 copy-start.22
  810.9 5.7 slice-start.2
  810.9 5.7 slice-start.3
  830.5 85.5 %reduce-scatter.23.cloned.1.call-start = ((), (), s32[]{:S(2)}) async-start(), calls=%async_computation.17 | async-start | bytes 2621440 | tf_op jit(solution)/shard_map/while/body/eval_jaxpr/reduce_scatter | solution.py:143
  836.7 8.9 copy-start.17
  836.7 8.8 copy-start.33
  836.7 8.8 copy-start.54
  848.6 9.6 copy-start.41
  850.7 7.5 copy-start.26
  858.2 27.7 %copy-start.37 = (f32[1024]{0:T(1024)S(1)}, f32[1024]{0:T(1024)}, u32[]{:S(2)}) copy-start(f32[1024]{0:T(1024)} %copy-done.36) | copy-start | bytes 12292 | tf_op jit(solution)/shard_map/while
  889.6 5.4 copy-start.27
  889.6 5.4 copy-start.39
  893.5 22.5 %copy-start.51 = (bf16[2,1024,256]{2,1,0:T(8,128)(2,1)S(1)}, bf16[2,1024,256]{2,1,0:T(8,128)(2,1)}, u32[]{:S(2)}) copy-start(bf16[2,1024,256]{2,1,0:T(8,128)(2,1)} %get-tuple-element.787) | copy-start | bytes 3145732 | tf_op jit(solution)/shard_map/while
  893.5 25.0 %copy-start.32 = (bf16[3,128,256]{1,2,0:T(8,128)(2,1)S(1)}, bf16[3,128,256]{1,2,0:T(8,128)(2,1)}, u32[]{:S(2)}) copy-start(bf16[3,128,256]{1,2,0:T(8,128)(2,1)} %copy-done.31) | copy-start | bytes 589828 | tf_op jit(solution)/shard_map/while
  893.7 23.8 %copy-start.44 = (f32[1024]{0:T(1024)}, f32[1024]{0:T(1024)S(1)}, u32[]{:S(2)}) copy-start(f32[1024]{0:T(1024)S(1)} %select_add_fusion.13) | copy-start | bytes 12292 | tf_op jit(solution)/shard_map/while
  895.2 22.4 %copy-start.28 = (f32[256,1024]{1,0:T(8,128)}, f32[256,1024]{1,0:T(8,128)S(1)}, u32[]{:S(2)}) copy-start(f32[256,1024]{1,0:T(8,128)S(1)} %select_add_fusion.12) | copy-start | bytes 3145732 | tf_op jit(solution)/shard_map/while
  921.4 66.5 %reduce-scatter.17.cloned.1.call-start = ((), (), s32[]{:S(2)}) async-start(), calls=%async_computation.8 | async-start | bytes 589824
  923.8 129.3 %reduce-scatter.21.cloned.1.call-start = ((), (), s32[]{:S(2)}) async-start(), calls=%async_computation.10 | async-start | bytes 589824
  926.2 194.8 %reduce-scatter.13.cloned.1.call-start = ((), (), s32[]{:S(2)}) async-start(), calls=%async_computation.6 | async-start | bytes 1769472 | tf_op jit(solution)/shard_map/reduce_scatter | solution.py:209
  929.3 262.4 %reduce-scatter.19.cloned.1.call-start = ((), (), s32[]{:S(2)}) async-start(), calls=%async_computation.9 | async-start | bytes 2359296
  934.5 327.9 %reduce-scatter.15.cloned.1.call-start = ((), (), s32[]{:S(2)}) async-start(), calls=%async_computation.7 | async-start | bytes 2359296 | tf_op jit(solution)/shard_map/reduce_scatter | solution.py:215
  (72 other events, 193.5 us)
Sparse Core Ops, SparseCore 0:
  12.6 52.2 all-gather.13
  127.9 48.5 all-reduce.6
  178.6 49.3 all-gather.11
  229.9 49.4 all-gather.15
  292.8 49.5 all-reduce.8
  377.2 51.4 all-reduce.10
  431.2 31.4 reduce-scatter.22
  468.8 49.3 all-gather.13
  582.0 47.7 all-reduce.6
  631.8 49.3 all-gather.11
  683.2 49.5 all-gather.15
  746.3 49.5 all-reduce.8
  830.7 51.4 all-reduce.10
  884.5 31.4 reduce-scatter.22
Sparse Core Ops, SparseCore 1:
  925.8 62.0 reduce-scatter.16
  992.1 61.0 reduce-scatter.20
  1056.4 64.5 reduce-scatter.12
  1125.0 66.7 reduce-scatter.18
  1195.7 66.7 reduce-scatter.14
where the time goes:
time: 1270 us
  waiting for transfers between devices  711 us (56%)
  blocking collectives  213 us (17%)
  matrix products  167 us (13%)
  other arithmetic  94.6 us (7%)
  local copies, waits for them, and re-layouts  60.8 us (5%)
  between operations  16.6 us (1%)
    unnamed x8, waiting for transfers between devices  159 us
    psum x2, waiting for transfers between devices, step(): lax.psum(d_n2_term.astype(jnp.bfloat16), 'tensor').astype(jnp.float32)  98.7 us
    all_gather x2, waiting for transfers between devices, step(): lax.all_gather(w_up, 'dp', axis=0, tiled=True)  91 us
    all_gather x2, waiting for transfers between devices, step(): lax.all_gather(w_down, 'dp', axis=1, tiled=True)  72.2 us
    reduce_scatter x1, waiting for transfers between devices, shards(): lax.psum_scatter(carry[2].astype(jnp.bfloat16), 'dp', scatter_dimension=0...  68.7 us
    reduce_scatter x1, waiting for transfers between devices, shards(): lax.psum_scatter(carry[0].astype(jnp.bfloat16), 'dp', scatter_dimension=1...  65.6 us
    all_gather x2, blocking collectives, step(): lax.all_gather(w_time, 'dp', axis=1, tiled=True)  59.9 us
    psum x2, waiting for transfers between devices, step(): lax.psum(attn_term.astype(jnp.bfloat16), 'tensor').astype(jnp.float32)  59.6 us
  transfers between devices with their start and end apart: 19, of which 17 were waited for; matrix products, arithmetic and copies ran while one was open for 12% of the time, Pallas kernels for 0%

commit v1 on v0

v1 whole, which is shorter than its diff:
```python
import math

import jax
import jax.numpy as jnp
from jax import lax
from jax.sharding import PartitionSpec as P

HEADS = 16
TEMB = 256
eps = 1e-05
masked = -1000000000.0
f32 = jnp.float32
bf16 = jnp.bfloat16


def sinusoid(values, width):
    half = width // 2
    freqs = jnp.exp(-math.log(10000.0) * jnp.arange(half, dtype=f32) / half)
    angles = values[..., None] * freqs
    return jnp.concatenate([jnp.sin(angles), jnp.cos(angles)], axis=-1)


def norm_parts(hidden):
    centre = jnp.mean(hidden, axis=-1, keepdims=True)
    centred = hidden - centre
    spread = jnp.mean(centred * centred, axis=-1, keepdims=True)
    inv = lax.rsqrt(spread + eps)
    return centred * inv, inv


def norm_back(unit, inv, gain, grad):
    scaled = grad * gain
    first = jnp.mean(scaled, axis=-1, keepdims=True)
    second = jnp.mean(scaled * unit, axis=-1, keepdims=True)
    return inv * (scaled - first - unit * second)


def positions(segs, offsets):
    seq_len = segs.shape[0]
    index = jnp.arange(seq_len, dtype=jnp.int32)
    member = segs[:, None] == jnp.arange(offsets.shape[0], dtype=jnp.int32)[None, :]
    starts = jnp.min(jnp.where(member, index[:, None], seq_len), axis=0)
    start_tok = jnp.sum(jnp.where(member, starts[None, :], 0), axis=1)
    offset_tok = jnp.sum(jnp.where(member, offsets[None, :], 0), axis=1)
    return offset_tok + index - start_tok


def attend(query, key, value, same, scale):
    scores = jnp.einsum("qhe,khe->hqk", query, key, preferred_element_type=f32) * scale
    scores = jnp.where(same[None], scores, masked)
    top = jnp.max(scores, axis=-1, keepdims=True)
    expo = jnp.exp(scores - top)
    denom = jnp.sum(expo, axis=-1, keepdims=True)
    probs = (expo / denom).astype(bf16)
    out = jnp.einsum("hqk,khe->qhe", probs, value, preferred_element_type=f32)
    return out, top + jnp.log(denom)


def attend_back(query, key, value, same, scale, lse, d_mixed):
    scores = jnp.einsum("qhe,khe->hqk", query, key, preferred_element_type=f32) * scale
    scores = jnp.where(same[None], scores, masked)
    probs = jnp.exp(scores - lse)
    d_probs = jnp.einsum("qhe,khe->hqk", d_mixed, value, preferred_element_type=f32)
    d_value = jnp.einsum("hqk,qhe->khe", probs.astype(bf16), d_mixed, preferred_element_type=f32)
    delta = jnp.sum(probs * d_probs, axis=-1, keepdims=True)
    d_scores = (probs * (d_probs - delta)).astype(bf16)
    d_query = jnp.einsum("hqk,khe->qhe", d_scores, key, preferred_element_type=f32) * scale
    d_key = jnp.einsum("hqk,qhe->khe", d_scores, query, preferred_element_type=f32) * scale
    return d_query, d_key, d_value


def mm(left, right):
    return jnp.dot(left, right, preferred_element_type=f32)


def mm_rt(left, right):
    return jnp.einsum("ik,jk->ij", left, right, preferred_element_type=f32)


def mm_lt(left, right):
    return jnp.einsum("ki,kj->ij", left, right, preferred_element_type=f32)


class Ring:
    def __init__(self, n):
        self.n = n
        self.order = list(range(0, n, 2)) + list(range(n - 1, 0, -2))
        inverse = [self.order.index(i) for i in range(n)]
        self.me = lax.axis_index("dp")
        self.spot = jnp.array(inverse, jnp.int32)[self.me]
        self.table = jnp.array(self.order, jnp.int32)
        self.right = [(self.order[p], self.order[(p + 1) % n]) for p in range(n)]
        self.left = [(b, a) for a, b in self.right]

    def at(self, offset):
        return self.table[(self.spot + offset) % self.n]

    def gather(self, block):
        rows = block.shape[0]
        full = jnp.zeros((self.n * rows,) + block.shape[1:], block.dtype)
        full = lax.dynamic_update_slice_in_dim(full, block, self.me * rows, 0)
        from_left = from_right = block
        for hop in range(1, self.n // 2 + 1):
            from_left = lax.ppermute(from_left, "dp", self.right)
            if hop <= self.n - 1 - self.n // 2:
                from_right = lax.ppermute(from_right, "dp", self.left)
                full = lax.dynamic_update_slice_in_dim(full, from_right, self.at(hop) * rows, 0)
            full = lax.dynamic_update_slice_in_dim(full, from_left, self.at(-hop) * rows, 0)
        return full

    def scatter(self, full):
        rows = full.shape[0] // self.n

        def part(offset):
            return lax.dynamic_slice_in_dim(full, self.at(offset) * rows, rows, 0).astype(f32)

        total = part(0)
        for hops, way, sign in (
            (self.n // 2, self.right, 1),
            (self.n - 1 - self.n // 2, self.left, -1),
        ):
            run = part(sign * hops)
            for hop in range(1, hops + 1):
                run = lax.ppermute(run.astype(bf16), "dp", way).astype(f32)
                if hop < hops:
                    run = run + part(sign * (hops - hop))
            if hops:
                total = total + run
        return total


def swap(value, bit, n):
    return lax.ppermute(value, "tensor", [(i, i ^ bit) for i in range(n)])


def to_features(value, n):
    me = lax.axis_index("tensor")
    tokens, width = value.shape
    value = value.reshape(tokens, n, width // n)
    bit = 1
    while bit < n:
        value = value.reshape(tokens, -1, 2, width // n)
        mine = (me // bit) % 2
        keep = lax.dynamic_index_in_dim(value, mine, 2, keepdims=False)
        send = lax.dynamic_index_in_dim(value, 1 - mine, 2, keepdims=False)
        got = swap(send.astype(bf16), bit, n).astype(f32)
        if bit == 1:
            got = jnp.concatenate([got[tokens // 2 :], got[: tokens // 2]], axis=0)
        value = keep.astype(f32) + got
        bit *= 2
    return value.reshape(tokens, width // n)


def shards(
    inputs,
    segment_ids,
    doc_offsets,
    time_index,
    w_qkv,
    w_out,
    w_up,
    w_down,
    w_time,
    gain_attn,
    gain_mlp,
    cotangent,
):
    n_dp = lax.axis_size("dp")
    n_tensor = lax.axis_size("tensor")
    me_dp = lax.axis_index("dp")
    core = lax.axis_index("tensor") % 2
    chips = n_tensor // 2
    seqs_dev, seq_len, width = inputs.shape
    half = seq_len // 2
    shard = width // n_tensor
    head_size = width // HEADS
    heads_dev = shard // head_size
    scale = head_size ** (-0.5)
    hidden_dev = w_up.shape[1]
    ring = Ring(n_dp)

    w1_part = jnp.concatenate([w_qkv[0], w_qkv[1], w_qkv[2], w_out.T], axis=1)
    w1 = ring.gather(w1_part)
    w2_part = jnp.concatenate([w_up, w_down.T], axis=1)
    w2 = lax.all_gather(w2_part, "dp", axis=0, tiled=True)

    times = lax.all_gather(time_index, "dp", axis=0, tiled=True)
    temb = sinusoid(times.astype(f32), TEMB)
    cond_part = jnp.dot(temb, w_time.astype(f32), precision=lax.Precision.HIGHEST)
    small = jnp.concatenate(
        [cond_part, gain_attn.astype(f32)[None], gain_mlp.astype(f32)[None]], axis=0
    )
    small = lax.all_gather(small, "dp", axis=1, tiled=True)
    n_seqs = n_dp * seqs_dev
    cond = lax.dynamic_slice_in_dim(small, me_dp * seqs_dev, seqs_dev, 0)
    attn_g, mlp_g = small[n_seqs], small[n_seqs + 1]

    def own_first(value):
        return jnp.roll(value, -core * half, axis=0)

    def exchange_core(value):
        return swap(value, 1, n_tensor)

    def sum_chips(value):
        bit = 2
        value = value.astype(f32)
        while bit < n_tensor:
            low = value.astype(bf16)
            value = low.astype(f32) + swap(low, bit, n_tensor).astype(f32)
            bit *= 2
        return value

    seqs = range(seqs_dev)
    cot = [own_first(cotangent[i]) for i in seqs]
    segs = [own_first(segment_ids[i]) for i in seqs]
    same = [s[:, None] == s[None, :] for s in segs]
    h0, unit0, inv0, n1 = [], [], [], []
    for i in seqs:
        place = own_first(positions(segment_ids[i], doc_offsets[i]))
        h = own_first(inputs[i]).astype(f32) + sinusoid(place.astype(f32), width) + cond[i][None]
        unit, inv = norm_parts(h)
        h0.append(h)
        unit0.append(unit)
        inv0.append(inv)
        n1.append((unit * attn_g).astype(bf16))
    query, key, value, mixed, lse = [], [], [], [], []
    h1, unit1, inv1, n2 = [], [], [], []
    for i in seqs:
        qkv = mm(n1[i], w1[:, : 3 * shard]).astype(bf16)
        heads = [
            qkv[:, c * shard : (c + 1) * shard].reshape(seq_len, heads_dev, head_size)
            for c in range(3)
        ]
        out, total = attend(*heads, same[i], scale)
        out = out.reshape(seq_len, shard).astype(bf16)
        send = mm_rt(out[half:], w1[:, 3 * shard :]).astype(bf16)
        keep = mm_rt(out[:half], w1[:, 3 * shard :]).astype(bf16)
        attn = sum_chips(keep.astype(f32) + exchange_core(send).astype(f32))
        h = h0[i][:half] + attn
        unit, inv = norm_parts(h)
        own = (unit * mlp_g).astype(bf16)
        query.append(heads[0])
        key.append(heads[1])
        value.append(heads[2])
        mixed.append(out)
        lse.append(total)
        h1.append(h)
        unit1.append(unit)
        inv1.append(inv)
        n2.append(jnp.concatenate([own, exchange_core(own)], axis=0))
    w_up_full, w_down_t = w2[:, :hidden_dev], w2[:, hidden_dev:]
    active, d_hidden, d_h1, d_h1_low, block_out = [], [], [], [], []
    gain_mlp_sum = jnp.zeros((width,), f32)
    for i in seqs:
        hidden = mm(n2[i], w_up_full)
        d_active = mm(cot[i], w_down_t)
        erf = lax.erf(hidden * (0.5**0.5))
        cdf = 0.5 + 0.5 * erf
        active.append((hidden * cdf).astype(bf16))
        slope = cdf + hidden * jnp.exp(-0.5 * hidden * hidden) * (0.5 / math.pi) ** 0.5
        d_hidden.append((d_active * slope).astype(bf16))
        d_n2_send = mm_rt(d_hidden[i][half:], w_up_full).astype(bf16)
        d_n2_keep = mm_rt(d_hidden[i][:half], w_up_full).astype(bf16)
        d_n2 = sum_chips(d_n2_keep.astype(f32) + exchange_core(d_n2_send).astype(f32))
        gain_mlp_sum = gain_mlp_sum + jnp.sum(d_n2 * unit1[i], axis=0)
        d_h1.append(cot[i][:half].astype(f32) + norm_back(unit1[i], inv1[i], mlp_g, d_n2))
        low = d_h1[i].astype(bf16)
        d_h1_low.append(jnp.concatenate([low, exchange_core(low)], axis=0))
        term = mm_rt(active[i], w_down_t)
        term = jnp.concatenate([term[:half] + h1[i] * (1.0 / chips), term[half:]], axis=0)
        block_out.append(to_features(term.astype(bf16), n_tensor).astype(bf16))
    cot_all = jnp.concatenate(cot, axis=0)
    grad2 = jnp.concatenate(
        [
            mm_lt(jnp.concatenate(n2, axis=0), jnp.concatenate(d_hidden, axis=0)).astype(bf16),
            mm_lt(cot_all, jnp.concatenate(active, axis=0)).astype(bf16),
        ],
        axis=1,
    )
    share2 = lax.psum_scatter(grad2, "dp", scatter_dimension=0, tiled=True).astype(f32)
    d_qkv, input_grad, seq_sums = [], [], []
    gain_attn_sum = jnp.zeros((width,), f32)
    for i in seqs:
        d_mixed = mm(d_h1_low[i], w1[:, 3 * shard :]).astype(bf16)
        parts = attend_back(
            query[i],
            key[i],
            value[i],
            same[i],
            scale,
            lse[i],
            d_mixed.reshape(seq_len, heads_dev, head_size),
        )
        d_qkv.append(
            jnp.concatenate([p.reshape(seq_len, shard).astype(bf16) for p in parts], axis=1)
        )
        d_n1 = mm_rt(d_qkv[i], w1[:, : 3 * shard])
        gain_attn_sum = gain_attn_sum + jnp.sum(d_n1 * unit0[i], axis=0)
        term = norm_back(unit0[i], inv0[i], attn_g, d_n1)
        term = jnp.concatenate([term[:half] + d_h1[i] * (1.0 / chips), term[half:]], axis=0)
        seq_sums.append(jnp.sum(term, axis=0))
        input_grad.append(to_features(term.astype(bf16), n_tensor))
    grad1 = jnp.concatenate(
        [
            mm_lt(jnp.concatenate(n1, axis=0), jnp.concatenate(d_qkv, axis=0)).astype(bf16),
            mm_lt(jnp.concatenate(d_h1_low, axis=0), jnp.concatenate(mixed, axis=0)).astype(bf16),
        ],
        axis=1,
    )
    share1 = ring.scatter(grad1)
    sums = jnp.zeros((n_seqs, width), f32)
    sums = lax.dynamic_update_slice_in_dim(sums, jnp.stack(seq_sums), me_dp * seqs_dev, 0)
    sums = jnp.concatenate(
        [sums, gain_attn_sum[None], gain_mlp_sum[None] * (1.0 / chips)], axis=0
    )
    sums = lax.psum(sums, ("dp", "tensor"))
    rows = width // n_dp
    sums = lax.dynamic_slice_in_dim(sums, me_dp * rows, rows, 1)
    factor = float(n_seqs * seq_len) ** (-0.5)
    grad_time = (
        jnp.einsum("st,sd->td", temb, sums[:n_seqs], precision=lax.Precision.HIGHEST) * factor
    )

    def natural(value):
        return jnp.roll(value, core * half, axis=0)

    share1, share2 = share1 * factor, share2 * factor
    return (
        jnp.stack([natural(b) for b in block_out]),
        jnp.stack([natural(g) for g in input_grad]),
        jnp.stack([share1[:, c * shard : (c + 1) * shard] for c in range(3)]),
        share1[:, 3 * shard :].T,
        share2[:, :hidden_dev],
        share2[:, hidden_dev:].T,
        grad_time,
        sums[n_seqs] * factor,
        sums[n_seqs + 1] * factor,
    )


def solution(mesh):
    in_specs = (
        P("dp", None, None),
        P("dp", None),
        P("dp", None),
        P("dp"),
        P(None, "dp", "tensor"),
        P("tensor", "dp"),
        P("dp", "tensor"),
        P("tensor", "dp"),
        P(None, "dp"),
        P("dp"),
        P("dp"),
        P("dp", None, None),
    )
    out_specs = (
        P("dp", None, "tensor"),
        P("dp", None, "tensor"),
        P(None, "dp", "tensor"),
        P("tensor", "dp"),
        P("dp", "tensor"),
        P("tensor", "dp"),
        P(None, "dp"),
        P("dp"),
        P("dp"),
    )
    return jax.shard_map(shards, mesh=mesh, in_specs=in_specs, out_specs=out_specs, check_vma=False)
```

time: 1270 us -> 692 us (0.54)
  waiting for transfers between devices: 711 us -> 223 us
  blocking collectives: 213 us -> 43.3 us
  local copies, waits for them, and re-layouts: 60.8 us -> 91.1 us
  starting transfers between devices: 1.77 us -> 30.1 us
  other arithmetic: 94.6 us -> 121 us
  matrix products: 167 us -> 145 us
  between operations: 16.6 us -> 30.1 us
    reduce_scatter x4 -> x0, waiting for transfers between devices: 176 us -> none  [the longest x1 68.7 us: shards(): lax.psum_scatter(carry[2].astype(jnp.bfloat16), 'dp', scatter_dimension=0...]
    all_gather x6 -> x1, waiting for transfers between devices: 163 us -> 0.01 us  [shards(): w2 = lax.all_gather(w2_part, 'dp', axis=0, tiled=True)]
    all_gather x8 -> x1, blocking collectives: 192 us -> 31.2 us  [shards(): small = lax.all_gather(small, 'dp', axis=1, tiled=True)]
    psum x6 -> x1, waiting for transfers between devices: 209 us -> 49.8 us  [shards(): sums = lax.psum(sums, ('dp', 'tensor'))]
    ppermute x0 -> x34, waiting for transfers between devices: none -> 125 us  [the longest x20 82.5 us: swap(): return lax.ppermute(value, 'tensor', [(i, i ^ bit) for i in range(n)])]
    unnamed x8 -> x4, waiting for transfers between devices: 159 us -> 47.9 us
    while x229 -> x0, local copies, waits for them, and re-layouts: 43.9 us -> none
    ppermute x0 -> x34, starting transfers between devices: none -> 30 us  [the longest x20 14.4 us: swap(): return lax.ppermute(value, 'tensor', [(i, i ^ bit) for i in range(n)])]
  transfers between devices with their start and end apart: 19 -> 37, of which waited for: 17 -> 18; matrix products, arithmetic and copies ran while one was open for 12% -> 36% of each run, Pallas kernels for 0% -> 0%
where the time goes in v1:
time: 692 us; the launch traced here: 684 us
  waiting for transfers between devices  223 us (32%)
  matrix products  145 us (21%)
  other arithmetic  121 us (17%)
  local copies, waits for them, and re-layouts  91.1 us (13%)
  blocking collectives  43.3 us (6%)
  starting transfers between devices  30.1 us (4%)
  between operations  30.1 us (4%)
    ppermute x20, waiting for transfers between devices, swap(): return lax.ppermute(value, 'tensor', [(i, i ^ bit) for i in range(n)])  82.5 us
    psum x1, waiting for transfers between devices, shards(): sums = lax.psum(sums, ('dp', 'tensor'))  49.8 us
    unnamed x4, waiting for transfers between devices  47.9 us
    unnamed x253, local copies, waits for them, and re-layouts  38.5 us
    ppermute x7, waiting for transfers between devices, scatter(): run = lax.ppermute(run.astype(bf16), 'dp', way).astype(f32)  35.6 us
    all_gather x1, blocking collectives, shards(): small = lax.all_gather(small, 'dp', axis=1, tiled=True)  31.2 us
    dot_general x8, matrix products, mm(): return jnp.dot(left, right, preferred_element_type=f32)  26.2 us
    dot_general x4, matrix products, mm_lt(): return jnp.einsum('ki,kj->ij', left, right, preferred_element_type=f32)  25 us
  transfers between devices with their start and end apart: 37, of which 18 were waited for; matrix products, arithmetic and copies ran while one was open for 36% of the time, Pallas kernels for 0%

profile of v1, /device:TPU:0, one launch (start us, length us, event | category | flops | bytes accessed | tf_op | source)
XLA Modules:
  0.0 683.8 jit_solution(16655282718602888327)
XLA Ops:
  9.1 3.0 collective-permute-start
  14.9 12.1 %all-reduce = s32[16]{0:T(128)S(1)} all-reduce(s32[16]{0:T(128)S(1)} %dynamic-update-slice), channel_id=1, replica_groups=mesh['dp'=8,'tensor'=4] {'dp'}, use_global_device_ids=true, to_apply=%add | all-reduce | flops 16 | bytes 128
  28.4 31.2 %all_gather.10 = f32[18,1024]{1,0:T(8,128)S(1)} all-gather(f32[18,128]{1,0:T(8,128)S(1)} %pad_maximum_fusion.10), channel_id=1, replica_groups=mesh['dp'=8,'tensor'=4] {'dp'}, dimensions={1}, use_global_device_ids=true | all-gather | bytes 82944 | tf_op jit(solution)/shard_map/all_gather | solution.py:193
  59.7 4.7 slice_bitcast_fusion.3
  64.4 16.2 %multiply_sine_fusion.1 = (f32[1024,512]{1,0:T(8,128)S(1)}, f32[1024,512]{1,0:T(8,128)S(1)}, f32[1024,512]{1,0:T(8,128)}, f32[1024,512]{1,0:T(8,128)}) fusion(f32[512]{0:T(512)S(1)} %multiply_exponential_fusion, f32[1024]{0:T(1024)S(1)} %get-tuple-element.168, f32[1024]{0:T(1024)S(1)} %get-tuple-element.166), kind=kLoop, calls=%fused_computation.119 | loop fusion | flops 1048576 | bytes 8398848 | tf_op jit(solution)/shard_map/sin | solution.py:20
  106.7 2.3 collective-permute-done.5
  110.7 4.9 collective-permute-done.6
  117.7 7.5 %fusion.238 = (f32[4,1024]{1,0:T(4,128)S(1)}, f32[4,1024,1024]{1,2,0:T(8,128)}) fusion(bf16[1024,4,64]{0,2,1:T(8,128)(2,1)S(1)} %bitcast.178, bf16[1024,4,64]{0,2,1:T(8,128)(2,1)S(1)} %bitcast.176, pred[1024,1024]{0,1:T(8,128)(4,1)S(1)} %broadcast_compare_fusion.1), kind=kOutput, calls=%fused_computation.439 | convolution fusion | flops 549449728 | bytes 18890752 | tf_op jit(solution)/shard_map/qhe,khe->hqk/dot_general | solution.py:49
  125.1 8.0 %fusion = f32[4,1024]{1,0:T(4,128)S(1)} fusion(f32[4,1024,1024]{1,2,0:T(8,128)} %get-tuple-element.152, f32[4,1024]{1,0:T(4,128)S(1)} %get-tuple-element.151), kind=kLoop, calls=%fused_computation.12 | loop fusion | flops 8384512 | bytes 16809984 | tf_op jit(solution)/shard_map/reduce_sum | solution.py:53
  133.2 7.6 %fusion.144 = bf16[4,64,1024]{2,1,0:T(8,128)(2,1)S(1)} fusion(bf16[1024,4,64]{0,2,1:T(8,128)(2,1)S(1)} %bitcast.188, f32[4,1024,1024]{1,2,0:T(8,128)} %get-tuple-element.152, f32[4,1024]{1,0:T(4,128)S(1)} %fusion, f32[4,1024]{1,0:T(4,128)S(1)} %get-tuple-element.151), kind=kOutput, calls=%fused_computation.250 | convolution fusion | flops 549715968 | bytes 17858560 | tf_op jit(solution)/shard_map/hqk,khe->qhe/dot_general | solution.py:55
  146.0 23.7 %collective-permute-done.8 = bf16[512,1024]{1,0:T(8,128)(2,1)S(1)} collective-permute-done((bf16[512,1024]{1,0:T(8,128)(2,1)S(1)}, bf16[512,1024]{1,0:T(8,128)(2,1)S(1)}, u32[]{:S(2)}, u32[]{:S(2)}) %collective-permute-start.8) | collective-permute-done | bytes 1048608 | tf_op jit(solution)/shard_map/ppermute | solution.py:133
  174.4 4.1 fusion.68
  178.6 4.7 multiply_convert_fusion.4
  183.3 3.7 fusion.17
  188.4 2.6 collective-permute-done.17
  193.9 3.1 fusion.225
  197.0 2.4 fusion.122
  203.0 2.9 copy.144
  205.9 11.9 %collective-permute-done.18 = bf16[512,1024]{1,0:T(8,128)(2,1)} collective-permute-done((bf16[512,1024]{1,0:T(8,128)(2,1)S(1)}, bf16[512,1024]{1,0:T(8,128)(2,1)}, u32[]{:S(2)}, u32[]{:S(2)}) %collective-permute-start.18) | collective-permute-done | bytes 1048608 | tf_op jit(solution)/shard_map/ppermute | solution.py:133
  217.7 2.7 multiply_reduce_fusion.11
  220.5 3.5 fusion.219
  226.7 2.6 fusion.133
  229.3 9.4 %fusion.124 = bf16[4,64,1024]{2,1,0:T(8,128)(2,1)} fusion(bf16[1024,4,64]{0,2,1:T(8,128)(2,1)S(1)} %bitcast.182, f32[4,1024,1024]{1,2,0:T(8,128)} %get-tuple-element.152, f32[4,1024]{1,0:T(4,128)S(1)} %log_add_fusion.1), kind=kOutput, calls=%fused_computation.240 | convolution fusion | flops 545521664 | bytes 17842176 | tf_op jit(solution)/shard_map/hqk,qhe->khe/dot_general | solution.py:64
  238.8 7.6 %multiply_reduce_fusion.1 = (f32[4,1024]{1,0:T(4,128)S(1)}, f32[4,1024,1024]{1,2,0:T(8,128)}) fusion(f32[4,1024,1024]{1,2,0:T(8,128)S(1)} %bitcast.171, f32[4,1024]{1,0:T(4,128)S(1)} %log_add_fusion.1, bf16[1024,4,64]{0,2,1:T(8,128)(2,1)S(1)} %bitcast.183, bf16[1024,4,64]{0,2,1:T(8,128)(2,1)S(1)} %bitcast.189), kind=kOutput, calls=%fused_computation.4 | convolution fusion | flops 549449728 | bytes 34635776 | tf_op jit(solution)/shard_map/qhe,khe->hqk/dot_general | solution.py:63
  246.4 8.0 %multiply_convert_fusion.1 = bf16[4,1024,1024]{1,2,0:T(8,128)(2,1)S(1)} fusion(f32[4,1024,1024]{1,2,0:T(8,128)} %get-tuple-element.156, f32[4,1024,1024]{1,2,0:T(8,128)S(1)} %bitcast.171, f32[4,1024]{1,0:T(4,128)S(1)} %get-tuple-element.155, f32[4,1024]{1,0:T(4,128)S(1)} %log_add_fusion.1), kind=kLoop, calls=%fused_computation.3 | loop fusion | flops 16777216 | bytes 41975808 | tf_op jit(solution)/shard_map/convert_element_type | solution.py:66
  254.5 2.7 fusion.137
  260.4 3.6 multiply_reduce_fusion.3
  264.0 3.5 subtract_multiply_fusion.1
  269.5 7.5 %fusion.239 = (f32[4,1024]{1,0:T(4,128)S(1)}, f32[4,1024,1024]{1,2,0:T(8,128)}) fusion(bf16[1024,4,64]{0,2,1:T(8,128)(2,1)S(1)} %bitcast.174, bf16[1024,4,64]{0,2,1:T(8,128)(2,1)S(1)} %bitcast.172, pred[1024,1024]{0,1:T(8,128)(4,1)S(1)} %broadcast_compare_fusion), kind=kOutput, calls=%fused_computation.440 | convolution fusion | flops 549449728 | bytes 18890752 | tf_op jit(solution)/shard_map/qhe,khe->hqk/dot_general | solution.py:49
  277.0 8.0 %fusion.1 = f32[4,1024]{1,0:T(4,128)S(1)} fusion(f32[4,1024,1024]{1,2,0:T(8,128)} %get-tuple-element.159, f32[4,1024]{1,0:T(4,128)S(1)} %get-tuple-element.158), kind=kLoop, calls=%fused_computation.13 | loop fusion | flops 8384512 | bytes 16809984 | tf_op jit(solution)/shard_map/reduce_sum | solution.py:53
  285.0 7.7 %fusion.143 = bf16[4,64,1024]{2,1,0:T(8,128)(2,1)S(1)} fusion(bf16[1024,4,64]{0,2,1:T(8,128)(2,1)S(1)} %bitcast.186, f32[4,1024,1024]{1,2,0:T(8,128)} %get-tuple-element.159, f32[4,1024]{1,0:T(4,128)S(1)} %fusion.1, f32[4,1024]{1,0:T(4,128)S(1)} %get-tuple-element.158), kind=kOutput, calls=%fused_computation.249 | convolution fusion | flops 549715968 | bytes 17858560 | tf_op jit(solution)/shard_map/hqk,khe->qhe/dot_general | solution.py:55
  298.0 23.7 %collective-permute-done.13 = bf16[512,1024]{1,0:T(8,128)(2,1)S(1)} collective-permute-done((bf16[512,1024]{1,0:T(8,128)(2,1)S(1)}, bf16[512,1024]{1,0:T(8,128)(2,1)S(1)}, u32[]{:S(2)}, u32[]{:S(2)}) %collective-permute-start.13) | collective-permute-done | bytes 1048608 | tf_op jit(solution)/shard_map/ppermute | solution.py:133
  323.8 4.7 fusion.67
  328.5 2.7 slice.402
  333.5 2.6 concatenate.137
  339.7 5.5 multiply_convert_fusion.2
  345.2 3.7 fusion.23
  355.7 3.0 concatenate.150
  358.7 2.6 concatenate.149
  366.2 3.9 add_convert_fusion
  371.6 2.4 fusion.120
  377.6 2.9 copy.145
  380.5 9.4 %fusion.89 = bf16[1024,1024]{0,1:T(8,128)(2,1)} fusion(bf16[1024,1024]{1,0:T(8,128)(2,1)} %get-tuple-element.160, bf16[1024,1024]{1,0:T(8,128)(2,1)} %copy-done.109, bf16[1024,1024]{1,0:T(8,128)(2,1)} %fusion.67, bf16[1024,1024]{1,0:T(8,128)(2,1)} %fusion.68), kind=kOutput, calls=%fused_computation.203 | convolution fusion | flops 4312793088 | bytes 10485760 | tf_op jit(solution)/shard_map/ki,kj->ij/dot_general | solution.py:81
  389.9 5.8 collective-permute-done.23
  395.7 2.5 multiply_reduce_fusion.10
  398.3 4.2 fusion.220
  402.6 9.2 %fusion.94 = bf16[1024,1024]{0,1:T(8,128)(2,1)} fusion(bf16[1024,1024]{1,0:T(8,128)(2,1)} %copy-done.108, bf16[1024,1024]{1,0:T(8,128)(2,1)} %copy-done.107, bf16[512,1024]{1,0:T(8,128)(2,1)} %collective-permute-done.14, bf16[512,1024]{1,0:T(8,128)(2,1)} %multiply_convert_fusion.6, bf16[512,1024]{1,0:T(8,128)(2,1)} %collective-permute-done.9, ...), kind=kOutput, calls=%fused_computation.204 | convolution fusion | flops 4321181696 | bytes 10485760 | tf_op jit(solution)/shard_map/ki,kj->ij/dot_general | solution.py:81
  414.9 3.6 fusion.127
  418.5 10.5 %multiply_reduce_fusion = (f32[4,1024]{1,0:T(4,128)S(1)}, f32[4,1024,1024]{1,2,0:T(8,128)}) fusion(f32[4,1024,1024]{1,2,0:T(8,128)S(1)} %bitcast.169, f32[4,1024]{1,0:T(4,128)S(1)} %log_add_fusion, bf16[1024,4,64]{0,2,1:T(8,128)(2,1)} %bitcast.185, bf16[1024,4,64]{0,2,1:T(8,128)(2,1)} %bitcast.187), kind=kOutput, calls=%fused_computation.1 | convolution fusion | flops 549449728 | bytes 34635776 | tf_op jit(solution)/shard_map/qhe,khe->hqk/dot_general | solution.py:63
  429.0 8.1 %multiply_convert_fusion = bf16[4,1024,1024]{1,2,0:T(8,128)(2,1)S(1)} fusion(f32[4,1024,1024]{1,2,0:T(8,128)} %get-tuple-element.163, f32[4,1024,1024]{1,2,0:T(8,128)S(1)} %bitcast.169, f32[4,1024]{1,0:T(4,128)S(1)} %get-tuple-element.162, f32[4,1024]{1,0:T(4,128)S(1)} %log_add_fusion), kind=kLoop, calls=%fused_computation | loop fusion | flops 16777216 | bytes 41975808 | tf_op jit(solution)/shard_map/convert_element_type | solution.py:66
  437.2 2.7 fusion.139
  442.3 2.8 multiply_reduce_fusion.2
  450.0 4.1 pad_maximum_fusion
  454.1 6.8 copy.139
  482.8 7.7 %collective-permute-done.21 = bf16[1024,1,256]{2,0,1:T(8,128)(2,1)} collective-permute-done((bf16[1024,1,256]{2,0,1:T(8,128)(2,1)}, bf16[1024,1,256]{2,0,1:T(8,128)(2,1)}, u32[]{:S(2)}, u32[]{:S(2)}) %collective-permute-start.21) | collective-permute-done | bytes 524320 | tf_op jit(solution)/shard_map/ppermute | solution.py:133
  493.1 2.8 slice.403
  498.9 2.9 fusion.140
  502.6 3.4 fusion.99
  512.6 2.7 collective-permute-done.27
  519.9 49.8 %all-reduce.3.cloned.1.call-done = f32[18,1024]{1,0:T(8,128)} async-done(((f32[18,1024]{1,0:T(8,128)}), f32[18,1024]{1,0:T(8,128)}) %all-reduce.3.cloned.1.call-update) | async-done | bytes 73744 | tf_op jit(solution)/shard_map/psum | solution.py:316
  572.6 3.3 collective-permute-start.29
  585.4 14.7 %collective-permute-done.32 = bf16[128,1024]{0,1:T(8,128)(2,1)S(1)} collective-permute-done((bf16[128,1024]{0,1:T(8,128)(2,1)S(1)}, bf16[128,1024]{0,1:T(8,128)(2,1)S(1)}, u32[]{:S(2)}, u32[]{:S(2)}) %collective-permute-start.32) | collective-permute-done | bytes 262176 | tf_op jit(solution)/shard_map/ppermute | solution.py:124
  604.2 16.3 %collective-permute-done.33 = bf16[128,1024]{0,1:T(8,128)(2,1)S(1)} collective-permute-done((bf16[128,1024]{0,1:T(8,128)(2,1)S(1)}, bf16[128,1024]{0,1:T(8,128)(2,1)S(1)}, u32[]{:S(2)}, u32[]{:S(2)}) %collective-permute-start.33) | collective-permute-done | bytes 262176 | tf_op jit(solution)/shard_map/ppermute | solution.py:124
  625.6 47.9 %reduce-scatter.4.cloned.1.call-done = bf16[128,2048]{1,0:T(8,128)(2,1)} async-done(((bf16[1024,2048]{1,0:T(8,128)(2,1)}), bf16[128,2048]{1,0:T(8,128)(2,1)}) %reduce-scatter.4.cloned.1.call-update) | async-done | bytes 524304
  (455 shorter events, 151.4 us)
Async XLA Ops:
  7.2 20.7 %copy-start = (bf16[256,128]{1,0:T(8,128)(2,1)S(1)}, bf16[256,128]{1,0:T(8,128)(2,1)}, u32[]{:S(2)}) copy-start(bf16[256,128]{1,0:T(8,128)(2,1)} %param.30) | copy-start | bytes 196612
  7.2 171.3 %all-gather.2.cloned.1.call-start = ((), (), s32[]{:S(2)}) async-start(), calls=%async_computation.1 | async-start | bytes 4718592 | tf_op jit(solution)/shard_map/all_gather | solution.py:185
  8.7 18.3 %copy-start.96 = (s32[2,8]{1,0:T(2,128)S(1)}, s32[2,8]{1,0:T(2,128)}, u32[]{:S(2)}) copy-start(s32[2,8]{1,0:T(2,128)} %param.24) | copy-start | bytes 196
  8.7 18.3 %copy-start.94 = (s32[2,1024]{1,0:T(2,128)S(1)}, s32[2,1024]{1,0:T(2,128)}, u32[]{:S(2)}) copy-start(s32[2,1024]{1,0:T(2,128)} %param.23) | copy-start | bytes 24580
  8.7 19.0 %copy-start.97 = (bf16[128]{0:T(256)(128)(2,1)S(1)}, bf16[128]{0:T(256)(128)(2,1)}, u32[]{:S(2)}) copy-start(bf16[128]{0:T(256)(128)(2,1)} %param.32) | copy-start | bytes 772
  8.7 19.0 %copy-start.98 = (bf16[128]{0:T(256)(128)(2,1)S(1)}, bf16[128]{0:T(256)(128)(2,1)}, u32[]{:S(2)}) copy-start(bf16[128]{0:T(256)(128)(2,1)} %param.31) | copy-start | bytes 772
  9.1 77.5 %collective-permute-start = (bf16[128,1024]{0,1:T(8,128)(2,1)S(1)}, bf16[128,1024]{0,1:T(8,128)(2,1)}, u32[]{:S(2)}, u32[]{:S(2)}) collective-permute-start(bf16[128,1024]{0,1:T(8,128)(2,1)S(1)} %get-tuple-element.117), channel_id=1, source_target_pairs={{8,0},{16,8},{24,16},{28,24},{20,28},{12,20},{4,12},{0,4},{9,1},{1... | collective-permute-start | bytes 786440 | tf_op jit(solution)/shard_map/ppermute | solution.py:106
  12.1 74.6 %collective-permute-start.1 = (bf16[128,1024]{0,1:T(8,128)(2,1)S(1)}, bf16[128,1024]{0,1:T(8,128)(2,1)S(1)}, u32[]{:S(2)}, u32[]{:S(2)}) collective-permute-start(bf16[128,1024]{0,1:T(8,128)(2,1)S(1)} %get-tuple-element.117), channel_id=1, source_target_pairs={{0,8},{8,16},{16,24},{24,28},{28,20},{20,12},{12,4},{4,0},{1,9},{9... | collective-permute-start | bytes 786440 | tf_op jit(solution)/shard_map/ppermute | solution.py:104
  13.3 556.4 %all-reduce.3.cloned.1.call-start = ((), (), s32[]{:S(2)}) async-start(), calls=%async_computation.2 | async-start | bytes 196608 | tf_op jit(solution)/shard_map/psum | solution.py:316
  64.4 16.3 %copy-start.25 = (bf16[1024,1024]{1,0:T(8,128)(2,1)S(1)}, bf16[1024,1024]{1,0:T(8,128)(2,1)}, u32[]{:S(2)}) copy-start(bf16[1024,1024]{1,0:T(8,128)(2,1)} %get-tuple-element.85) | copy-start | bytes 6291460
  84.7 12.5 %copy-start.92 = (s32[8]{0:T(128)S(1)}, s32[8]{0:T(128)}, u32[]{:S(2)}) copy-start(s32[8]{0:T(128)} %constant.326.clone) | copy-start | bytes 100
  86.6 17.2 %collective-permute-start.2 = (bf16[128,1024]{0,1:T(8,128)(2,1)}, bf16[128,1024]{0,1:T(8,128)(2,1)}, u32[]{:S(2)}, u32[]{:S(2)}) collective-permute-start(bf16[128,1024]{0,1:T(8,128)(2,1)} %collective-permute-done), channel_id=1, source_target_pairs={{8,0},{16,8},{24,16},{28,24},{20,28},{12,20},{4,12},{0,4},{9,1},{1... | collective-permute-start | bytes 786440 | tf_op jit(solution)/shard_map/ppermute | solution.py:106
  86.6 15.7 %collective-permute-start.3 = (bf16[128,1024]{0,1:T(8,128)(2,1)S(1)}, bf16[128,1024]{0,1:T(8,128)(2,1)}, u32[]{:S(2)}, u32[]{:S(2)}) collective-permute-start(bf16[128,1024]{0,1:T(8,128)(2,1)S(1)} %collective-permute-done.1), channel_id=1, source_target_pairs={{0,8},{8,16},{16,24},{24,28},{28,20},{20,12},{12,4},{4,0},{1,9},{9... | collective-permute-start | bytes 786440 | tf_op jit(solution)/shard_map/ppermute | solution.py:104
  102.4 13.3 %copy-start.59 = (bf16[1024,1024]{1,0:T(8,128)(2,1)S(1)}, bf16[1024,1024]{1,0:T(8,128)(2,1)}, u32[]{:S(2)}) copy-start(bf16[1024,1024]{1,0:T(8,128)(2,1)} %multiply_convert_fusion.5) | copy-start | bytes 6291460
  102.4 6.6 collective-permute-start.5
  103.8 6.6 collective-permute-start.4
  109.0 6.5 collective-permute-start.6
  115.7 25.7 %copy-start.14 = (bf16[1024,1024]{0,1:T(8,128)(2,1)}, bf16[1024,1024]{0,1:T(8,128)(2,1)S(1)}, u32[]{:S(2)}) copy-start(bf16[1024,1024]{0,1:T(8,128)(2,1)S(1)} %constant_dynamic-update-slice_fusion.1) | copy-start | bytes 6291460
  117.7 15.5 %copy-start.57 = (bf16[1024,256]{0,1:T(8,128)(2,1)}, bf16[1024,256]{0,1:T(8,128)(2,1)S(1)}, u32[]{:S(2)}) copy-start(bf16[1024,256]{0,1:T(8,128)(2,1)S(1)} %get-tuple-element.95) | copy-start | bytes 1572868
  141.3 2.7 collective-permute-start.7
  141.4 28.3 %copy-start.6 = (f32[1024,1024]{1,0:T(8,128)S(1)}, f32[1024,1024]{1,0:T(8,128)}, u32[]{:S(2)}) copy-start(f32[1024,1024]{1,0:T(8,128)} %copy-done.5) | copy-start | bytes 12582916
  144.4 25.3 %collective-permute-start.8 = (bf16[512,1024]{1,0:T(8,128)(2,1)S(1)}, bf16[512,1024]{1,0:T(8,128)(2,1)S(1)}, u32[]{:S(2)}, u32[]{:S(2)}) collective-permute-start(bf16[512,1024]{1,0:T(8,128)(2,1)S(1)} %add_convert_fusion.5), channel_id=1, source_target_pairs={{0,2},{1,3},{2,0},{3,1},{4,6},{5,7},{6,4},{7,5},{8,10},{9,11},{10,... | collective-permute-start | bytes 3145736 | tf_op jit(solution)/shard_map/ppermute | solution.py:133
  170.8 7.7 %collective-permute-start.9 = (bf16[512,1024]{1,0:T(8,128)(2,1)S(1)}, bf16[512,1024]{1,0:T(8,128)(2,1)}, u32[]{:S(2)}, u32[]{:S(2)}) collective-permute-start(bf16[512,1024]{1,0:T(8,128)(2,1)S(1)} %multiply_convert_fusion.7), channel_id=1, source_target_pairs={{0,1},{1,0},{2,3},{3,2},{4,5},{5,4},{6,7},{7,6},{8,9},{9,8},{10,11... | collective-permute-start | bytes 3145736 | tf_op jit(solution)/shard_map/ppermute | solution.py:133
  183.3 13.7 %copy-start.109 = (bf16[1024,1024]{1,0:T(8,128)(2,1)}, bf16[1024,1024]{1,0:T(8,128)(2,1)S(1)}, u32[]{:S(2)}) copy-start(bf16[1024,1024]{1,0:T(8,128)(2,1)S(1)} %get-tuple-element.153) | copy-start | bytes 6291460
  188.4 2.7 collective-permute-start.17
  192.4 25.4 %collective-permute-start.18 = (bf16[512,1024]{1,0:T(8,128)(2,1)S(1)}, bf16[512,1024]{1,0:T(8,128)(2,1)}, u32[]{:S(2)}, u32[]{:S(2)}) collective-permute-start(bf16[512,1024]{1,0:T(8,128)(2,1)S(1)} %add_convert_fusion.1), channel_id=1, source_target_pairs={{0,2},{1,3},{2,0},{3,1},{4,6},{5,7},{6,4},{7,5},{8,10},{9,11},{10,... | collective-permute-start | bytes 3145736 | tf_op jit(solution)/shard_map/ppermute | solution.py:133
  205.9 14.6 %copy-start.19 = (f32[512,1024]{1,0:T(8,128)S(1)}, f32[512,1024]{1,0:T(8,128)}, u32[]{:S(2)}) copy-start(f32[512,1024]{1,0:T(8,128)} %copy.144) | copy-start | bytes 6291460
  205.9 14.6 %copy-start.40 = (bf16[1024,1024]{1,0:T(8,128)(2,1)S(1)}, bf16[1024,1024]{1,0:T(8,128)(2,1)}, u32[]{:S(2)}) copy-start(bf16[1024,1024]{1,0:T(8,128)(2,1)} %fusion.68) | copy-start | bytes 6291460
  220.5 18.3 %slice-start.4 = ((s8[16777216]{0:T(1024)(128)(4,1)}), s8[4194304]{0:T(1024)(128)(4,1)S(1)}, s32[]{:S(2)}) async-start(s8[16777216]{0:T(1024)(128)(4,1)} %bitcast.170), calls=%async_computation.8 | async-start | bytes 8388608
  220.5 18.3 %slice-start.5 = ((s8[16777216]{0:T(1024)(128)(4,1)}), s8[4194304]{0:T(1024)(128)(4,1)S(1)}, s32[]{:S(2)}) async-start(s8[16777216]{0:T(1024)(128)(4,1)} %bitcast.170), calls=%async_computation.9 | async-start | bytes 8388608
  224.0 2.7 collective-permute-start.19
  225.3 13.4 %slice-start.6 = ((s8[16777216]{0:T(1024)(128)(4,1)}), s8[4194304]{0:T(1024)(128)(4,1)S(1)}, s32[]{:S(2)}) async-start(s8[16777216]{0:T(1024)(128)(4,1)} %bitcast.170), calls=%async_computation.10 | async-start | bytes 8388608
  229.3 9.4 %slice-start.7 = ((s8[16777216]{0:T(1024)(128)(4,1)}), s8[4194304]{0:T(1024)(128)(4,1)S(1)}, s32[]{:S(2)}) async-start(s8[16777216]{0:T(1024)(128)(4,1)} %bitcast.170), calls=%async_computation.11 | async-start | bytes 8388608
  269.5 15.5 %copy-start.56 = (bf16[1024,256]{0,1:T(8,128)(2,1)}, bf16[1024,256]{0,1:T(8,128)(2,1)S(1)}, u32[]{:S(2)}) copy-start(bf16[1024,256]{0,1:T(8,128)(2,1)S(1)} %get-tuple-element.98) | copy-start | bytes 1572868
  293.3 2.7 collective-permute-start.12
  296.4 25.3 %collective-permute-start.13 = (bf16[512,1024]{1,0:T(8,128)(2,1)S(1)}, bf16[512,1024]{1,0:T(8,128)(2,1)S(1)}, u32[]{:S(2)}, u32[]{:S(2)}) collective-permute-start(bf16[512,1024]{1,0:T(8,128)(2,1)S(1)} %add_convert_fusion.3), channel_id=1, source_target_pairs={{0,2},{1,3},{2,0},{3,1},{4,6},{5,7},{6,4},{7,5},{8,10},{9,11},{10,... | collective-permute-start | bytes 3145736 | tf_op jit(solution)/shard_map/ppermute | solution.py:133
  323.8 15.6 %collective-permute-start.14 = (bf16[512,1024]{1,0:T(8,128)(2,1)}, bf16[512,1024]{1,0:T(8,128)(2,1)}, u32[]{:S(2)}, u32[]{:S(2)}) collective-permute-start(bf16[512,1024]{1,0:T(8,128)(2,1)} %multiply_convert_fusion.6), channel_id=1, source_target_pairs={{0,1},{1,0},{2,3},{3,2},{4,5},{5,4},{6,7},{7,6},{8,9},{9,8},{10,11... | collective-permute-start | bytes 3145736 | tf_op jit(solution)/shard_map/ppermute | solution.py:133
  339.0 121.9 %collective-permute-start.10 = (bf16[1024,2,256]{2,0,1:T(8,128)(2,1)}, bf16[1024,2,256]{2,0,1:T(8,128)(2,1)}, u32[]{:S(2)}, u32[]{:S(2)}) collective-permute-start(bf16[1024,2,256]{2,0,1:T(8,128)(2,1)} %fusion.154), channel_id=1, source_target_pairs={{0,1},{1,0},{2,3},{3,2},{4,5},{5,4},{6,7},{7,6},{8,9},{9,8},{10,11... | collective-permute-start | bytes 3145736 | tf_op jit(solution)/shard_map/ppermute | solution.py:133
  351.2 14.6 %collective-permute-start.22 = (bf16[512,1024]{1,0:T(8,128)(2,1)}, bf16[512,1024]{1,0:T(8,128)(2,1)}, u32[]{:S(2)}, u32[]{:S(2)}) collective-permute-start(bf16[512,1024]{1,0:T(8,128)(2,1)} %convolution_convert_fusion.2), channel_id=1, source_target_pairs={{0,1},{1,0},{2,3},{3,2},{4,5},{5,4},{6,7},{7,6},{8,9},{9,8},{10,11... | collective-permute-start | bytes 3145736 | tf_op jit(solution)/shard_map/ppermute | solution.py:133
  365.3 100.1 %collective-permute-start.20 = (bf16[1024,2,256]{2,0,1:T(8,128)(2,1)}, bf16[1024,2,256]{2,0,1:T(8,128)(2,1)}, u32[]{:S(2)}, u32[]{:S(2)}) collective-permute-start(bf16[1024,2,256]{2,0,1:T(8,128)(2,1)} %dynamic-slice_bitcast_fusion.1), channel_id=1, source_target_pairs={{0,1},{1,0},{2,3},{3,2},{4,5},{5,4},{6,7},{7,6},{8,9},{9,8},{10,11... | collective-permute-start | bytes 3145736 | tf_op jit(solution)/shard_map/ppermute | solution.py:133
  370.1 25.7 %collective-permute-start.23 = (bf16[512,1024]{1,0:T(8,128)(2,1)}, bf16[512,1024]{1,0:T(8,128)(2,1)}, u32[]{:S(2)}, u32[]{:S(2)}) collective-permute-start(bf16[512,1024]{1,0:T(8,128)(2,1)} %add_convert_fusion), channel_id=1, source_target_pairs={{0,2},{1,3},{2,0},{3,1},{4,6},{5,7},{6,4},{7,5},{8,10},{9,11},{10,... | collective-permute-start | bytes 3145736 | tf_op jit(solution)/shard_map/ppermute | solution.py:133
  398.3 16.6 %slice-start = ((s8[16777216]{0:T(1024)(128)(4,1)}), s8[4194304]{0:T(1024)(128)(4,1)S(1)}, s32[]{:S(2)}) async-start(s8[16777216]{0:T(1024)(128)(4,1)} %bitcast.168), calls=%async_computation.4 | async-start | bytes 8388608
  402.5 12.4 %slice-start.1 = ((s8[16777216]{0:T(1024)(128)(4,1)}), s8[4194304]{0:T(1024)(128)(4,1)S(1)}, s32[]{:S(2)}) async-start(s8[16777216]{0:T(1024)(128)(4,1)} %bitcast.168), calls=%async_computation.5 | async-start | bytes 8388608
  402.5 12.4 %slice-start.2 = ((s8[16777216]{0:T(1024)(128)(4,1)}), s8[4194304]{0:T(1024)(128)(4,1)S(1)}, s32[]{:S(2)}) async-start(s8[16777216]{0:T(1024)(128)(4,1)} %bitcast.168), calls=%async_computation.6 | async-start | bytes 8388608
  402.5 12.4 %slice-start.3 = ((s8[16777216]{0:T(1024)(128)(4,1)}), s8[4194304]{0:T(1024)(128)(4,1)S(1)}, s32[]{:S(2)}) async-start(s8[16777216]{0:T(1024)(128)(4,1)} %bitcast.168), calls=%async_computation.7 | async-start | bytes 8388608
  402.5 9.3 %collective-permute-start.24 = (bf16[512,1024]{1,0:T(8,128)(2,1)}, bf16[512,1024]{1,0:T(8,128)(2,1)}, u32[]{:S(2)}, u32[]{:S(2)}) collective-permute-start(bf16[512,1024]{1,0:T(8,128)(2,1)} %get-tuple-element.71), channel_id=1, source_target_pairs={{0,1},{1,0},{2,3},{3,2},{4,5},{5,4},{6,7},{7,6},{8,9},{9,8},{10,11... | collective-permute-start | bytes 3145736 | tf_op jit(solution)/shard_map/ppermute | solution.py:133
  449.7 223.8 %reduce-scatter.4.cloned.1.call-start = ((), (), s32[]{:S(2)}) async-start(), calls=%async_computation.3 | async-start | bytes 4718592
  464.0 15.1 %collective-permute-start.11 = (bf16[1024,1,256]{2,0,1:T(8,128)(2,1)}, bf16[1024,1,256]{2,0,1:T(8,128)(2,1)}, u32[]{:S(2)}, u32[]{:S(2)}) collective-permute-start(bf16[1024,1,256]{2,0,1:T(8,128)(2,1)} %dynamic-slice_convert_fusion.3), channel_id=1, source_target_pairs={{0,2},{1,3},{2,0},{3,1},{4,6},{5,7},{6,4},{7,5},{8,10},{9,11},{10,... | collective-permute-start | bytes 1572872 | tf_op jit(solution)/shard_map/ppermute | solution.py:133
  472.8 23.1 %collective-permute-start.15 = (bf16[1024,2,256]{2,0,1:T(8,128)(2,1)}, bf16[1024,2,256]{2,0,1:T(8,128)(2,1)S(1)}, u32[]{:S(2)}, u32[]{:S(2)}) collective-permute-start(bf16[1024,2,256]{2,0,1:T(8,128)(2,1)} %fusion.150), channel_id=1, source_target_pairs={{0,1},{1,0},{2,3},{3,2},{4,5},{5,4},{6,7},{7,6},{8,9},{9,8},{10,11... | collective-permute-start | bytes 3145736 | tf_op jit(solution)/shard_map/ppermute | solution.py:133
  475.5 15.0 %collective-permute-start.21 = (bf16[1024,1,256]{2,0,1:T(8,128)(2,1)}, bf16[1024,1,256]{2,0,1:T(8,128)(2,1)}, u32[]{:S(2)}, u32[]{:S(2)}) collective-permute-start(bf16[1024,1,256]{2,0,1:T(8,128)(2,1)} %dynamic-slice_convert_fusion.1), channel_id=1, source_target_pairs={{0,2},{1,3},{2,0},{3,1},{4,6},{5,7},{6,4},{7,5},{8,10},{9,11},{10,... | collective-permute-start | bytes 1572872 | tf_op jit(solution)/shard_map/ppermute | solution.py:133
  477.7 12.8 %copy-start.29 = (f32[1024,2,256]{2,0,1:T(8,128)S(1)}, f32[1024,2,256]{2,0,1:T(8,128)}, u32[]{:S(2)}) copy-start(f32[1024,2,256]{2,0,1:T(8,128)} %maximum_add_fusion.4) | copy-start | bytes 6291460
  497.3 80.0 %collective-permute-start.16 = (bf16[1024,1,256]{2,0,1:T(8,128)(2,1)}, bf16[1024,1,256]{2,0,1:T(8,128)(2,1)}, u32[]{:S(2)}, u32[]{:S(2)}) collective-permute-start(bf16[1024,1,256]{2,0,1:T(8,128)(2,1)} %dynamic-slice_convert_fusion.2), channel_id=1, source_target_pairs={{0,2},{1,3},{2,0},{3,1},{4,6},{5,7},{6,4},{7,5},{8,10},{9,11},{10,... | collective-permute-start | bytes 1572872 | tf_op jit(solution)/shard_map/ppermute | solution.py:133
  507.0 8.2 %collective-permute-start.27 = (bf16[128,1024]{0,1:T(8,128)(2,1)}, bf16[128,1024]{0,1:T(8,128)(2,1)}, u32[]{:S(2)}, u32[]{:S(2)}) collective-permute-start(bf16[128,1024]{0,1:T(8,128)(2,1)} %get-tuple-element.89), channel_id=1, source_target_pairs={{0,8},{8,16},{16,24},{24,28},{28,20},{20,12},{12,4},{4,0},{1,9},{9... | collective-permute-start | bytes 786440 | tf_op jit(solution)/shard_map/ppermute | solution.py:124
  507.2 71.2 %collective-permute-start.31 = (bf16[128,1024]{0,1:T(8,128)(2,1)}, bf16[128,1024]{0,1:T(8,128)(2,1)S(1)}, u32[]{:S(2)}, u32[]{:S(2)}) collective-permute-start(bf16[128,1024]{0,1:T(8,128)(2,1)} %get-tuple-element.90), channel_id=1, source_target_pairs={{8,0},{16,8},{24,16},{28,24},{20,28},{12,20},{4,12},{0,4},{9,1},{1... | collective-permute-start | bytes 786440 | tf_op jit(solution)/shard_map/ppermute | solution.py:124
  517.0 52.7 %copy-start.88 = (f32[16,128]{1,0:T(8,128)S(1)}, f32[16,128]{1,0:T(8,128)}, u32[]{:S(2)}) copy-start(f32[16,128]{1,0:T(8,128)} %copy-done.87) | copy-start | bytes 24580
  517.0 52.7 %copy-start.90 = (f32[16,128]{1,0:T(8,128)S(1)}, f32[16,128]{1,0:T(8,128)}, u32[]{:S(2)}) copy-start(f32[16,128]{1,0:T(8,128)} %copy-done.89) | copy-start | bytes 24580
  517.0 54.6 %collective-permute-start.28 = (bf16[128,1024]{0,1:T(8,128)(2,1)}, bf16[128,1024]{0,1:T(8,128)(2,1)}, u32[]{:S(2)}, u32[]{:S(2)}) collective-permute-start(bf16[128,1024]{0,1:T(8,128)(2,1)} %add_convert_fusion.12), channel_id=1, source_target_pairs={{0,8},{8,16},{16,24},{24,28},{28,20},{20,12},{12,4},{4,0},{1,9},{9... | collective-permute-start | bytes 786440 | tf_op jit(solution)/shard_map/ppermute | solution.py:124
  519.9 80.4 %collective-permute-start.25 = (bf16[1024,2,256]{2,0,1:T(8,128)(2,1)}, bf16[1024,2,256]{2,0,1:T(8,128)(2,1)S(1)}, u32[]{:S(2)}, u32[]{:S(2)}) collective-permute-start(bf16[1024,2,256]{2,0,1:T(8,128)(2,1)} %dynamic-slice_bitcast_fusion), channel_id=1, source_target_pairs={{0,1},{1,0},{2,3},{3,2},{4,5},{5,4},{6,7},{7,6},{8,9},{9,8},{10,11... | collective-permute-start | bytes 3145736 | tf_op jit(solution)/shard_map/ppermute | solution.py:133
  572.6 7.8 %collective-permute-start.29 = (bf16[128,1024]{0,1:T(8,128)(2,1)S(1)}, bf16[128,1024]{0,1:T(8,128)(2,1)S(1)}, u32[]{:S(2)}, u32[]{:S(2)}) collective-permute-start(bf16[128,1024]{0,1:T(8,128)(2,1)S(1)} %add_convert_fusion.11), channel_id=1, source_target_pairs={{0,8},{8,16},{16,24},{24,28},{28,20},{20,12},{12,4},{4,0},{1,9},{9... | collective-permute-start | bytes 786440 | tf_op jit(solution)/shard_map/ppermute | solution.py:124
  580.6 19.5 %collective-permute-start.32 = (bf16[128,1024]{0,1:T(8,128)(2,1)S(1)}, bf16[128,1024]{0,1:T(8,128)(2,1)S(1)}, u32[]{:S(2)}, u32[]{:S(2)}) collective-permute-start(bf16[128,1024]{0,1:T(8,128)(2,1)S(1)} %get-tuple-element.88), channel_id=1, source_target_pairs={{8,0},{16,8},{24,16},{28,24},{20,28},{12,20},{4,12},{0,4},{9,1},{1... | collective-permute-start | bytes 786440 | tf_op jit(solution)/shard_map/ppermute | solution.py:124
  584.8 19.4 %collective-permute-start.30 = (bf16[128,1024]{0,1:T(8,128)(2,1)S(1)}, bf16[128,1024]{0,1:T(8,128)(2,1)S(1)}, u32[]{:S(2)}, u32[]{:S(2)}) collective-permute-start(bf16[128,1024]{0,1:T(8,128)(2,1)S(1)} %get-tuple-element.87), channel_id=1, source_target_pairs={{0,8},{8,16},{16,24},{24,28},{28,20},{20,12},{12,4},{4,0},{1,9},{9... | collective-permute-start | bytes 786440 | tf_op jit(solution)/shard_map/ppermute | solution.py:124
  600.2 20.2 %collective-permute-start.33 = (bf16[128,1024]{0,1:T(8,128)(2,1)S(1)}, bf16[128,1024]{0,1:T(8,128)(2,1)S(1)}, u32[]{:S(2)}, u32[]{:S(2)}) collective-permute-start(bf16[128,1024]{0,1:T(8,128)(2,1)S(1)} %add_convert_fusion.8), channel_id=1, source_target_pairs={{8,0},{16,8},{24,16},{28,24},{20,28},{12,20},{4,12},{0,4},{9,1},{1... | collective-permute-start | bytes 786440 | tf_op jit(solution)/shard_map/ppermute | solution.py:124
  602.1 18.5 %copy-start.30 = (f32[1024,2,256]{2,0,1:T(8,128)}, f32[1024,2,256]{2,0,1:T(8,128)S(1)}, u32[]{:S(2)}) copy-start(f32[1024,2,256]{2,0,1:T(8,128)S(1)} %maximum_add_fusion.5) | copy-start | bytes 6291460
  602.1 20.1 %collective-permute-start.26 = (bf16[1024,1,256]{2,0,1:T(8,128)(2,1)S(1)}, bf16[1024,1,256]{2,0,1:T(8,128)(2,1)S(1)}, u32[]{:S(2)}, u32[]{:S(2)}) collective-permute-start(bf16[1024,1,256]{2,0,1:T(8,128)(2,1)S(1)} %dynamic-slice_convert_fusion), channel_id=1, source_target_pairs={{0,2},{1,3},{2,0},{3,1},{4,6},{5,7},{6,4},{7,5},{8,10},{9,11},{10,... | collective-permute-start | bytes 1572872 | tf_op jit(solution)/shard_map/ppermute | solution.py:133
  (92 other events, 350.7 us)
Sparse Core Ops, SparseCore 0:
  13.4 80.6 all-gather.1
  449.9 119.7 all-reduce.2
  573.3 100.1 reduce-scatter.3

commit v2 on v1

v2 whole, which is shorter than its diff:
```python
import functools
import math

import jax
import jax.numpy as jnp
from jax import lax
from jax.experimental import pallas as pl
from jax.experimental.pallas import tpu as pltpu
from jax.sharding import PartitionSpec as P

HEADS = 16
TEMB = 256
BLOCK = 256
LANES = 128
eps = 1e-05
masked = -1000000000.0
f32 = jnp.float32
bf16 = jnp.bfloat16
VMEM = pl.BlockSpec(memory_space=pltpu.VMEM)
SMEM = pl.BlockSpec(memory_space=pltpu.SMEM)
params = pltpu.CompilerParams(vmem_limit_bytes=56 * 1024 * 1024)


def freqs(width):
    half = width // 2
    return jnp.exp(-math.log(10000.0) * jnp.arange(half, dtype=f32) / half)


def sinusoid(values, width):
    angles = values[..., None] * freqs(width)
    return jnp.concatenate([jnp.sin(angles), jnp.cos(angles)], axis=-1)


def norm_parts(hidden):
    centre = jnp.mean(hidden, axis=-1, keepdims=True)
    centred = hidden - centre
    spread = jnp.mean(centred * centred, axis=-1, keepdims=True)
    inv = lax.rsqrt(spread + eps)
    return centred * inv, inv


def norm_back(unit, inv, gain, grad):
    scaled = grad * gain
    first = jnp.mean(scaled, axis=-1, keepdims=True)
    second = jnp.mean(scaled * unit, axis=-1, keepdims=True)
    return inv * (scaled - first - unit * second)


def positions(segs, offsets):
    seq_len = segs.shape[0]
    index = jnp.arange(seq_len, dtype=jnp.int32)
    member = segs[:, None] == jnp.arange(offsets.shape[0], dtype=jnp.int32)[None, :]
    starts = jnp.min(jnp.where(member, index[:, None], seq_len), axis=0)
    start_tok = jnp.sum(jnp.where(member, starts[None, :], 0), axis=1)
    offset_tok = jnp.sum(jnp.where(member, offsets[None, :], 0), axis=1)
    return offset_tok + index - start_tok


def dot(left, right, left_dim, right_dim):
    return lax.dot_general(
        left, right, (((left_dim,), (right_dim,)), ((), ())), preferred_element_type=f32
    )


def like(shape, dtype):
    return jax.ShapeDtypeStruct(shape, dtype)


def rows_at(block):
    return pl.ds(pl.multiple_of(block * BLOCK, BLOCK), BLOCK)


def exchanged(core, block, blocks):
    return lax.rem(block + core * (blocks // 2), blocks)


def embed_kernel(meta, x, place, freq, out):
    half = freq.shape[1]
    angles = place[...].astype(f32) * freq[...]
    out[:, :half] = x[:, :half].astype(f32) + jnp.sin(angles)
    out[:, half:] = x[:, half:].astype(f32) + jnp.cos(angles)


def embedded(meta, x, place):
    seq_len, width = x.shape
    blocks = seq_len // BLOCK

    def source(i, m):
        return (exchanged(m[0], i, blocks), 0)

    return pl.pallas_call(
        embed_kernel,
        out_shape=like((seq_len, width), f32),
        grid_spec=pltpu.PrefetchScalarGridSpec(
            num_scalar_prefetch=1,
            grid=(blocks,),
            in_specs=[
                pl.BlockSpec((BLOCK, width), source),
                pl.BlockSpec((BLOCK, 1), source),
                pl.BlockSpec((1, width // 2), lambda i, m: (0, 0)),
            ],
            out_specs=pl.BlockSpec((BLOCK, width), lambda i, m: (i, 0)),
        ),
        compiler_params=params,
        name="embed",
    )(meta, x, place[:, None], freqs(width)[None])


def first_norm_kernel(x, cond, gain, h0, n1):
    h = x[...] + cond[...]
    unit, inv = norm_parts(h)
    h0[...] = h
    n1[...] = (unit * gain[...]).astype(bf16)


def first_norm(x, cond, gain):
    seq_len, width = x.shape
    row = pl.BlockSpec((BLOCK, width), lambda i: (i, 0))
    one = pl.BlockSpec((1, width), lambda i: (0, 0))
    return pl.pallas_call(
        first_norm_kernel,
        grid=(seq_len // BLOCK,),
        out_shape=(like(x.shape, f32), like(x.shape, bf16)),
        in_specs=[row, one, one],
        out_specs=(row, row),
        compiler_params=params,
        name="first_norm",
    )(x, cond, gain)


def window(meta, block, blocks):
    first, last = meta[1 + block], meta[1 + blocks + block]
    low, high = jnp.int32(blocks), jnp.int32(0)
    for j in range(blocks):
        hit = (meta[1 + blocks + j] >= first) & (meta[1 + j] <= last)
        low = jnp.where(hit & (low == blocks), j, low)
        high = jnp.where(hit, j + 1, high)
    return low, high - low


def set_bias(bias, seg_col, seg_row, block, low, count):
    keys = jnp.concatenate([seg_row[pl.ds(low + j, 1), :] for j in range(count)], axis=1)
    bias[:, : count * BLOCK] = jnp.where(seg_col[rows_at(block), :] == keys, 0.0, masked)


def attend_kernel(shard, scale, meta, n1, w1, seg_col, seg_row, qkv, a, lse, keep, send, bias):
    seq_len = n1.shape[0]
    blocks = seq_len // BLOCK
    half = seq_len // 2

    def project(block, _):
        terms = dot(n1[rows_at(block), :], w1[:, : 3 * shard], 1, 0)
        qkv[rows_at(exchanged(meta[0], block, blocks)), :] = terms.astype(bf16)
        return 0

    lax.fori_loop(0, blocks, project, 0)
    even = lax.broadcasted_iota(jnp.int32, (BLOCK, LANES), 1) < LANES // 2

    def attend(block, _):
        own = rows_at(exchanged(meta[0], block, blocks))
        low, count = window(meta, block, blocks)
        for size in range(1, blocks + 1):

            @pl.when(count == size)
            def _(size=size):
                span = size * BLOCK
                keys = pl.ds(pl.multiple_of(low * BLOCK, BLOCK), span)
                set_bias(bias, seg_col, seg_row, block, low, size)
                for pair in range(shard // LANES):
                    at = pair * LANES
                    query = qkv[rows_at(block), at : at + LANES] * jnp.bfloat16(scale)
                    key = qkv[keys, shard + at : shard + at + LANES]
                    value = qkv[keys, 2 * shard + at : 2 * shard + at + LANES]
                    outs = []
                    for e in range(2):
                        picked = jnp.where(even == (e == 0), query, jnp.bfloat16(0))
                        scores = dot(picked, key, 1, 1) + bias[:, :span]
                        top = jnp.max(scores, axis=1, keepdims=True)
                        expo = jnp.exp(scores - top)
                        denom = jnp.sum(expo, axis=1, keepdims=True)
                        outs.append(dot(expo.astype(bf16), value, 1, 0) * (1.0 / denom))
                        head = 2 * pair + e
                        lse[rows_at(block), head : head + 1] = top + jnp.log(denom)
                    a[own, at : at + LANES] = jnp.where(even, outs[0], outs[1]).astype(bf16)

        return 0

    lax.fori_loop(0, blocks, attend, 0)

    def project_out(block, _):
        w_out_t = w1[:, 3 * shard :]
        send[rows_at(block), :] = dot(a[rows_at(block + blocks // 2), :], w_out_t, 1, 1).astype(bf16)
        keep[rows_at(block), :] = dot(a[rows_at(block), :], w_out_t, 1, 1).astype(bf16)
        return 0

    lax.fori_loop(0, half // BLOCK, project_out, 0)


def attended(meta, n1, w1, seg_col, seg_row, shard, scale):
    seq_len, width = n1.shape
    return pl.pallas_call(
        functools.partial(attend_kernel, shard, scale),
        out_shape=(
            like((seq_len, 3 * shard), bf16),
            like((seq_len, shard), bf16),
            like((seq_len, LANES), f32),
            like((seq_len // 2, width), bf16),
            like((seq_len // 2, width), bf16),
        ),
        in_specs=[SMEM] + [VMEM] * 4,
        out_specs=(VMEM,) * 5,
        scratch_shapes=[pltpu.VMEM((BLOCK, seq_len), f32)],
        compiler_params=params,
        name="attend",
    )(meta, n1, w1, seg_col, seg_row)


def hidden_kernel(share, own, meta, n2, cot, w2, *refs):
    if own:
        h1, act, d_hid, d_n2, keep, send = refs
    else:
        act, d_hid, d_n2, keep, send = refs[-5:]
    hid = act.shape[1]
    chunk = min(512, hid)
    for at in range(0, hid, chunk):
        u = dot(n2[...], w2[:, at : at + chunk], 1, 0)
        d_act = dot(cot[...], w2[:, hid + at : hid + at + chunk], 1, 0)
        cdf = 0.5 + 0.5 * lax.erf(u * (0.5**0.5))
        act[:, at : at + chunk] = (u * cdf).astype(bf16)
        slope = cdf + u * (jnp.exp(-0.5 * u * u) * (0.5 / math.pi) ** 0.5)
        d_hid[:, at : at + chunk] = (d_act * slope).astype(bf16)
    d_n2[...] = dot(d_hid[...], w2[:, :hid], 1, 1).astype(bf16)
    term = dot(act[...], w2[:, hid:], 1, 1)
    if own:
        term = term + h1[...] * share
    split_features(meta[0], term.astype(bf16), keep, send)


def split_features(core, term, keep, send):
    groups, _, part = keep.shape
    for g in range(groups):
        first = term[:, 2 * g * part : (2 * g + 1) * part]
        second = term[:, (2 * g + 1) * part : (2 * g + 2) * part]
        keep[g] = jnp.where(core == 0, first, second)
        send[g] = jnp.where(core == 0, second, first)


def hidden_layer(meta, n2, cot, w2, h1, earlier, seq, seqs, share, groups):
    own = h1 is not None
    half, width = n2.shape
    hid = w2.shape[1] // 2
    per = half // BLOCK
    part = width // (2 * groups)
    base = (0 if own else per) + 2 * per * seq

    def cot_rows(i, m):
        return ((m[0] if own else 1 - m[0]) * per + i, 0)

    row = pl.BlockSpec((BLOCK, width), lambda i, m: (i, 0))
    placed = pl.BlockSpec((BLOCK, hid), lambda i, m: (base + i, 0))
    split = pl.BlockSpec((groups, BLOCK, part), lambda i, m: (0, (0 if own else per) + i, 0))
    ins = [n2, cot, w2]
    specs = [
        row,
        pl.BlockSpec((BLOCK, width), cot_rows),
        pl.BlockSpec(w2.shape, lambda i, m: (0, 0)),
    ]
    if own:
        ins.append(h1)
        specs.append(row)
    outs = {0: 0, 1: 1, 2: 3, 3: 4}
    aliases = {}
    for k, buffer in enumerate(earlier):
        aliases[1 + len(ins)] = outs[k]
        ins.append(buffer)
        specs.append(pl.BlockSpec(memory_space=pl.ANY))
    tokens = 2 * half
    return pl.pallas_call(
        functools.partial(hidden_kernel, share, own)
        if own and not earlier
        else functools.partial(hidden_skip, share, own, len(earlier)),
        out_shape=(
            like((seqs * tokens, hid), bf16),
            like((seqs * tokens, hid), bf16),
            like((half, width), bf16),
            like((groups, tokens, part), bf16),
            like((groups, tokens, part), bf16),
        ),
        grid_spec=pltpu.PrefetchScalarGridSpec(
            num_scalar_prefetch=1,
            grid=(per,),
            in_specs=specs,
            out_specs=(placed, placed, row, split, split),
        ),
        input_output_aliases=aliases,
        compiler_params=params,
        name="hidden_layer",
    )(meta, *ins)


def hidden_skip(share, own, count, meta, n2, cot, w2, *refs):
    if own:
        hidden_kernel(share, own, meta, n2, cot, w2, refs[0], *refs[1 + count :])
    else:
        hidden_kernel(share, own, meta, n2, cot, w2, *refs[count:])


def attend_back_kernel(
    shard,
    scale,
    meta,
    low_own,
    low_other,
    w1,
    qkv,
    a,
    lse,
    seg_col,
    seg_row,
    h0,
    d_h1,
    gain,
    d_qkv,
    keep,
    send,
    sums,
    d_mix,
    total,
    bias,
):
    seq_len = a.shape[0]
    blocks = seq_len // BLOCK
    per = blocks // 2

    def mix(block, _):
        w_out_t = w1[:, 3 * shard :]
        d_mix[rows_at(block), :] = dot(low_own[rows_at(block), :], w_out_t, 1, 0).astype(bf16)
        d_mix[rows_at(block + per), :] = dot(low_other[rows_at(block), :], w_out_t, 1, 0).astype(
            bf16
        )
        return 0

    lax.fori_loop(0, per, mix, 0)
    total[...] = jnp.zeros(total.shape, f32)
    even = lax.broadcasted_iota(jnp.int32, (BLOCK, LANES), 1) < LANES // 2

    def attend(block, _):
        own = rows_at(exchanged(meta[0], block, blocks))
        low, count = window(meta, block, blocks)
        for size in range(1, blocks + 1):

            @pl.when(count == size)
            def _(size=size):
                span = size * BLOCK
                keys = pl.ds(pl.multiple_of(low * BLOCK, BLOCK), span)
                set_bias(bias, seg_col, seg_row, block, low, size)
                for pair in range(shard // LANES):
                    at = pair * LANES
                    query = qkv[rows_at(block), at : at + LANES] * jnp.bfloat16(scale)
                    key = qkv[keys, shard + at : shard + at + LANES]
                    value = qkv[keys, 2 * shard + at : 2 * shard + at + LANES]
                    grad = d_mix[own, at : at + LANES]
                    product = grad.astype(f32) * a[own, at : at + LANES].astype(f32)
                    d_query = []
                    d_key = d_value = 0.0
                    for e in range(2):
                        side = even == (e == 0)
                        picked = jnp.where(side, query, jnp.bfloat16(0))
                        picked_grad = jnp.where(side, grad, jnp.bfloat16(0))
                        delta = jnp.sum(jnp.where(side, product, 0.0), axis=1, keepdims=True)
                        head = 2 * pair + e
                        scores = dot(picked, key, 1, 1) + bias[:, :span]
                        probs = jnp.exp(scores - lse[rows_at(block), head : head + 1])
                        d_probs = dot(picked_grad, value, 1, 1)
                        d_scores = (probs * (d_probs - delta)).astype(bf16)
                        d_query.append(dot(d_scores, key, 1, 0))
                        d_key = d_key + dot(d_scores, picked, 0, 0)
                        d_value = d_value + dot(probs.astype(bf16), picked_grad, 0, 0)
                    total[keys, at : at + LANES] += d_key
                    total[keys, shard + at : shard + at + LANES] += d_value
                    d_qkv[own, at : at + LANES] = (
                        jnp.where(even, d_query[0], d_query[1]) * scale
                    ).astype(bf16)

        return 0

    lax.fori_loop(0, blocks, attend, 0)
    share = 1.0 / keep.shape[0]
    sums[...] = jnp.zeros(sums.shape, f32)

    def back(block, _):
        rows = rows_at(block)
        d_qkv[rows, shard:] = total[rows_at(exchanged(meta[0], block, blocks)), :].astype(bf16)
        d_n1 = dot(d_qkv[rows, :], w1[:, : 3 * shard], 1, 1)
        unit, inv = norm_parts(h0[rows, :])
        sums[0:1, :] += jnp.sum(d_n1 * unit, axis=0, keepdims=True)
        term = norm_back(unit, inv, gain[...], d_n1)
        weight = jnp.where(block < per, share, 0.0)
        term = term + weight * d_h1[rows_at(lax.rem(block, per)), :]
        sums[1:2, :] += jnp.sum(term, axis=0, keepdims=True)
        split_features(meta[0], term.astype(bf16), keep.at[:, rows, :], send.at[:, rows, :])
        return 0

    lax.fori_loop(0, blocks, back, 0)


def attended_back(meta, low_own, low_other, w1, kept, seg_col, seg_row, h0, d_h1, gain, scale, groups):
    qkv, a, lse = kept
    seq_len, shard = a.shape
    width = w1.shape[0]
    part = width // (2 * groups)
    return pl.pallas_call(
        functools.partial(attend_back_kernel, shard, scale),
        out_shape=(
            like((seq_len, 3 * shard), bf16),
            like((groups, seq_len, part), bf16),
            like((groups, seq_len, part), bf16),
            like((8, width), f32),
        ),
        in_specs=[SMEM] + [VMEM] * 11,
        out_specs=(VMEM,) * 4,
        scratch_shapes=[
            pltpu.VMEM((seq_len, shard), bf16),
            pltpu.VMEM((seq_len, 2 * shard), f32),
            pltpu.VMEM((BLOCK, seq_len), f32),
        ],
        compiler_params=params,
        name="attend_back",
    )(meta, low_own, low_other, w1, qkv, a, lse, seg_col, seg_row, h0, d_h1, gain)


def mm_lt(left, right):
    return jnp.einsum("ki,kj->ij", left, right, preferred_element_type=f32)


class Ring:
    def __init__(self, n):
        self.n = n
        self.order = list(range(0, n, 2)) + list(range(n - 1, 0, -2))
        inverse = [self.order.index(i) for i in range(n)]
        self.me = lax.axis_index("dp")
        self.spot = jnp.array(inverse, jnp.int32)[self.me]
        self.table = jnp.array(self.order, jnp.int32)
        self.right = [(self.order[p], self.order[(p + 1) % n]) for p in range(n)]
        self.left = [(b, a) for a, b in self.right]

    def at(self, offset):
        return self.table[(self.spot + offset) % self.n]

    def gather(self, block):
        rows = block.shape[0]
        full = jnp.zeros((self.n * rows,) + block.shape[1:], block.dtype)
        full = lax.dynamic_update_slice_in_dim(full, block, self.me * rows, 0)
        from_left = from_right = block
        for hop in range(1, self.n // 2 + 1):
            from_left = lax.ppermute(from_left, "dp", self.right)
            if hop <= self.n - 1 - self.n // 2:
                from_right = lax.ppermute(from_right, "dp", self.left)
                full = lax.dynamic_update_slice_in_dim(full, from_right, self.at(hop) * rows, 0)
            full = lax.dynamic_update_slice_in_dim(full, from_left, self.at(-hop) * rows, 0)
        return full

    def scatter(self, full):
        rows = full.shape[0] // self.n

        def part(offset):
            return lax.dynamic_slice_in_dim(full, self.at(offset) * rows, rows, 0).astype(f32)

        total = part(0)
        for hops, way, sign in (
            (self.n // 2, self.right, 1),
            (self.n - 1 - self.n // 2, self.left, -1),
        ):
            run = part(sign * hops)
            for hop in range(1, hops + 1):
                run = lax.ppermute(run.astype(bf16), "dp", way).astype(f32)
                if hop < hops:
                    run = run + part(sign * (hops - hop))
            if hops:
                total = total + run
        return total


def swap(value, bit, n):
    return lax.ppermute(value, "tensor", [(i, i ^ bit) for i in range(n)])


def to_features(keep, send, n):
    chip = lax.axis_index("tensor") // 2
    half = keep.shape[1] // 2
    got = swap(send, 1, n)
    got = jnp.concatenate([got[:, half:], got[:, :half]], axis=1)
    value = keep.astype(f32) + got.astype(f32)
    bit = 1
    while 2 * bit < n:
        value = value.reshape((-1, 2) + value.shape[1:])
        mine = (chip // bit) % 2
        kept = lax.dynamic_index_in_dim(value, mine, 1, keepdims=False)
        sent = lax.dynamic_index_in_dim(value, 1 - mine, 1, keepdims=False)
        value = kept + swap(sent.astype(bf16), 2 * bit, n).astype(f32)
        bit *= 2
    return value[0]


def shards(
    inputs,
    segment_ids,
    doc_offsets,
    time_index,
    w_qkv,
    w_out,
    w_up,
    w_down,
    w_time,
    gain_attn,
    gain_mlp,
    cotangent,
):
    n_dp = lax.axis_size("dp")
    n_tensor = lax.axis_size("tensor")
    me_dp = lax.axis_index("dp")
    core = lax.axis_index("tensor") % 2
    chips = n_tensor // 2
    seqs_dev, seq_len, width = inputs.shape
    half = seq_len // 2
    blocks = seq_len // BLOCK
    shard = width // n_tensor
    scale = (width // HEADS) ** (-0.5)
    hidden_dev = w_up.shape[1]
    rows = width // n_dp
    n_seqs = n_dp * seqs_dev
    ring = Ring(n_dp)
    seqs = range(seqs_dev)

    marks = jnp.stack([time_index // 32, time_index % 32]).astype(bf16).reshape(1, -1)
    extra = jnp.concatenate(
        [
            gain_attn[:, None],
            gain_mlp[:, None],
            jnp.broadcast_to(marks, (rows, 2 * seqs_dev)),
            jnp.zeros((rows, LANES - 2 - 2 * seqs_dev), bf16),
        ],
        axis=1,
    )
    small = ring.gather(jnp.concatenate([w_time.T, extra], axis=1))
    w1 = ring.gather(jnp.concatenate([w_qkv[0], w_qkv[1], w_qkv[2], w_out.T], axis=1))
    w2 = lax.all_gather(jnp.concatenate([w_up, w_down.T], axis=1), "dp", axis=0, tiled=True)

    metas, seg_cols, seg_rows, entered = [], [], [], []
    for i in seqs:
        ids = segment_ids[i]
        metas.append(
            jnp.concatenate([core[None].astype(jnp.int32), ids[::BLOCK], ids[BLOCK - 1 :: BLOCK]])
        )
        seg_cols.append(ids[:, None])
        seg_rows.append(ids.reshape(blocks, BLOCK))
        entered.append(embedded(metas[i], inputs[i], positions(ids, doc_offsets[i])))
    temb = sinusoid(time_index.astype(f32), TEMB)
    cond = jnp.sum(temb[:, None, :] * small[None, :, :TEMB].astype(f32), axis=2)
    attn_g = small[:, TEMB].astype(f32)[None]
    mlp_g = small[:, TEMB + 1].astype(f32)[None]
    marks = small[::rows, TEMB + 2 : TEMB + 2 + 2 * seqs_dev].astype(f32)
    times = (marks[:, :seqs_dev] * 32 + marks[:, seqs_dev:]).reshape(n_seqs)

    def exchange_core(value):
        return swap(value, 1, n_tensor)

    def sum_chips(value):
        bit = 2
        while bit < n_tensor:
            low = value.astype(bf16)
            value = low.astype(f32) + swap(low, bit, n_tensor).astype(f32)
            bit *= 2
        return value

    h0, n1, kept, h1, unit1, inv1, n2 = [], [], [], [], [], [], []
    for i in seqs:
        h, n = first_norm(entered[i], cond[i : i + 1], attn_g)
        h0.append(h)
        n1.append(n)
    for i in seqs:
        qkv, a, lse, keep, send = attended(
            metas[i], n1[i], w1, seg_cols[i], seg_rows[i], shard, scale
        )
        kept.append((qkv, a, lse))
        attn = sum_chips(keep.astype(f32) + exchange_core(send).astype(f32))
        h = h0[i][:half] + attn
        unit, inv = norm_parts(h)
        own = (unit * mlp_g).astype(bf16)
        h1.append(h)
        unit1.append(unit)
        inv1.append(inv)
        n2.append((own, exchange_core(own)))
    share = 1.0 / chips
    buffers = ()
    d_h1, d_low, block_out = [], [], []
    gain_mlp_sum = jnp.zeros((1, width), f32)
    for i in seqs:
        act, d_hid, d_keep, keep, send = hidden_layer(
            metas[i], n2[i][0], cotangent[i], w2, h1[i], buffers, i, seqs_dev, share, chips
        )
        act, d_hid, d_send, keep, send = hidden_layer(
            metas[i],
            n2[i][1],
            cotangent[i],
            w2,
            None,
            (act, d_hid, keep, send),
            i,
            seqs_dev,
            share,
            chips,
        )
        buffers = (act, d_hid)
        d_n2 = sum_chips(d_keep.astype(f32) + exchange_core(d_send).astype(f32))
        gain_mlp_sum = gain_mlp_sum + jnp.sum(d_n2 * unit1[i], axis=0, keepdims=True)
        cot_own = lax.dynamic_slice_in_dim(cotangent[i], core * half, half, 0).astype(f32)
        d_h1.append(cot_own + norm_back(unit1[i], inv1[i], mlp_g, d_n2))
        low = d_h1[i].astype(bf16)
        d_low.append((low, exchange_core(low)))
        block_out.append(to_features(keep, send, n_tensor).astype(bf16))
    act, d_hid = buffers
    cot_all = jnp.concatenate([jnp.roll(cotangent[i], -core * half, axis=0) for i in seqs])
    grad2 = jnp.concatenate(
        [
            mm_lt(jnp.concatenate([x for pair in n2 for x in pair]), d_hid).astype(bf16),
            mm_lt(cot_all, act).astype(bf16),
        ],
        axis=1,
    )
    share2 = ring.scatter(grad2)
    d_qkv, input_grad, seq_sums = [], [], []
    gain_attn_sum = jnp.zeros((1, width), f32)
    for i in seqs:
        d, keep, send, sums = attended_back(
            metas[i],
            d_low[i][0],
            d_low[i][1],
            w1,
            kept[i],
            seg_cols[i],
            seg_rows[i],
            h0[i],
            d_h1[i],
            attn_g,
            scale,
            chips,
        )
        d_qkv.append(d)
        gain_attn_sum = gain_attn_sum + sums[0:1]
        seq_sums.append(sums[1:2])
        input_grad.append(to_features(keep, send, n_tensor))
    sums = jnp.zeros((LANES, width), f32)
    sums = lax.dynamic_update_slice_in_dim(sums, jnp.concatenate(seq_sums), me_dp * seqs_dev, 0)
    sums = lax.dynamic_update_slice_in_dim(
        sums, jnp.concatenate([gain_attn_sum, gain_mlp_sum * share]), n_seqs, 0
    )
    grad1 = jnp.concatenate(
        [
            mm_lt(jnp.concatenate(n1), jnp.concatenate(d_qkv)).astype(bf16),
            mm_lt(
                jnp.concatenate([x for pair in d_low for x in pair]),
                jnp.concatenate([k[1] for k in kept]),
            ).astype(bf16),
            sums.T.astype(bf16),
        ],
        axis=1,
    )
    share1 = ring.scatter(grad1)
    sums = share1[:, 4 * shard :]
    bit = 1
    while bit < n_tensor:
        sums = sums + swap(sums, bit, n_tensor)
        bit *= 2
    factor = float(n_seqs * seq_len) ** (-0.5)
    temb_all = sinusoid(times, TEMB)
    grad_time = (
        jnp.einsum("st,ds->td", temb_all, sums[:, :n_seqs], precision=lax.Precision.HIGHEST)
        * factor
    )

    def natural(value):
        return jnp.roll(value, core * half, axis=0)

    cols = 3 * shard
    return (
        jnp.stack([natural(b) for b in block_out]),
        jnp.stack([natural(g) for g in input_grad]),
        jnp.stack([share1[:, c * shard : (c + 1) * shard] for c in range(3)]) * factor,
        share1[:, cols : cols + shard].T * factor,
        share2[:, :hidden_dev] * factor,
        share2[:, hidden_dev:].T * factor,
        grad_time,
        sums[:, n_seqs] * factor,
        sums[:, n_seqs + 1] * factor,
    )


def solution(mesh):
    in_specs = (
        P("dp", None, None),
        P("dp", None),
        P("dp", None),
        P("dp"),
        P(None, "dp", "tensor"),
        P("tensor", "dp"),
        P("dp", "tensor"),
        P("tensor", "dp"),
        P(None, "dp"),
        P("dp"),
        P("dp"),
        P("dp", None, None),
    )
    out_specs = (
        P("dp", None, "tensor"),
        P("dp", None, "tensor"),
        P(None, "dp", "tensor"),
        P("tensor", "dp"),
        P("dp", "tensor"),
        P("tensor", "dp"),
        P(None, "dp"),
        P("dp"),
        P("dp"),
    )
    return jax.shard_map(shards, mesh=mesh, in_specs=in_specs, out_specs=out_specs, check_vma=False)
```

time: 692 us -> 522 us (0.75)
  Pallas kernels: 0 us -> 147 us
  matrix products: 145 us -> 22.4 us
  other arithmetic: 121 us -> 59.8 us
  waiting for transfers between devices: 223 us -> 165 us
  local copies, waits for them, and re-layouts: 91.1 us -> 39.8 us
  blocking collectives: 43.3 us -> 0 us
  starting transfers between devices: 30.1 us -> 50.4 us
    pallas_call x0 -> x12, Pallas kernels: none -> 147 us  [the longest x2 46.7 us: attended_back(): pl.pallas_call(functools.partial(attend_back_kernel, shard, scale), out_s...]
    dot_general x34 -> x1, matrix products: 120 us -> 1.05 us  [shards(): jnp.einsum('st,ds->td', temb_all, sums[:, :n_seqs], precision=lax.Precisi...]
    psum x1 -> x0, waiting for transfers between devices: 49.8 us -> none  [shards(): sums = lax.psum(sums, ('dp', 'tensor'))]
    unnamed x4 -> x1, waiting for transfers between devices: 47.9 us -> 0.02 us
    unnamed x253 -> x92, local copies, waits for them, and re-layouts: 38.5 us -> 7.14 us
    all_gather x1 -> x0, blocking collectives: 31.2 us -> none  [shards(): small = lax.all_gather(small, 'dp', axis=1, tiled=True)]
    ppermute x20 -> x22, waiting for transfers between devices: 82.5 us -> 114 us  [swap(): return lax.ppermute(value, 'tensor', [(i, i ^ bit) for i in range(n)])]
    reduce_sum x10 -> x3, other arithmetic: 24.8 us -> 3.47 us  [the longest x2 3.12 us: shards(): jnp.sum(d_n2 * unit1[i], axis=0, keepdims=True)]
  transfers between devices with their start and end apart: 37 -> 51, of which waited for: 18 -> 21; matrix products, arithmetic and copies ran while one was open for 36% -> 22% of each run, Pallas kernels for 0% -> 29%
where the time goes in v2:
time: 522 us; the launch traced here: 514 us
  waiting for transfers between devices  165 us (32%)
  Pallas kernels  147 us (28%)
  other arithmetic  59.8 us (11%)
  starting transfers between devices  50.4 us (10%)
  local copies, waits for them, and re-layouts  39.8 us (8%)
  between operations  28.5 us (5%)
  matrix products  22.4 us (4%)
    ppermute x22, waiting for transfers between devices, swap(): return lax.ppermute(value, 'tensor', [(i, i ^ bit) for i in range(n)])  114 us
    pallas_call x2, Pallas kernels, attended_back(): pl.pallas_call(functools.partial(attend_back_kernel, shard, scale), out_s...  46.7 us
    pallas_call x4, Pallas kernels, hidden_layer(): pl.pallas_call(functools.partial(hidden_kernel, share, own) if own and (n...  37.5 us
    pallas_call x2, Pallas kernels, attended(): pl.pallas_call(functools.partial(attend_kernel, shard, scale), out_shape=...  30.1 us
    ppermute x14, waiting for transfers between devices, scatter(): run = lax.ppermute(run.astype(bf16), 'dp', way).astype(f32)  25.8 us
    pallas_call x2, Pallas kernels, embedded(): pl.pallas_call(embed_kernel, out_shape=like((seq_len, width), f32), grid_...  22 us
    dot_general x4, matrix products, mm_lt(): return jnp.einsum('ki,kj->ij', left, right, preferred_element_type=f32)  21.4 us
    ppermute x8, waiting for transfers between devices, gather(): from_left = lax.ppermute(from_left, 'dp', self.right)  19.2 us
  transfers between devices with their start and end apart: 51, of which 21 were waited for; matrix products, arithmetic and copies ran while one was open for 22% of the time, Pallas kernels for 29%

profile of v2, /device:TPU:0, one launch (start us, length us, event | category | flops | bytes accessed | tf_op | source)
XLA Modules:
  0.0 513.7 jit_solution(15244008565360858840)
XLA Ops:
  8.2 1.9 concatenate.74
  10.0 3.0 collective-permute-start
  16.1 1.9 collective-permute-start.7
  21.0 4.7 slice_bitcast_fusion.1
  43.1 1.9 sub.88.place
  45.0 11.0 %embed.2.x = f32[1024,1024]{1,0:T(8,128)} custom-call(s32[9]{0:T(128)} %pad_add_fusion.meta, bf16[1024,1024]{1,0:T(8,128)(2,1)} %get-tuple-element.162.x, s32[1024,1]{1,0:T(8,128)} %sub.88.place, f32[1,512]{1,0:T(1,128)} %multiply_exponential_fusion.freq), custom_call_target="tpu_custom_call" | custom-call | tf_op jit(solution)/shard_map/embed/pallas_call | solution.py:91
  57.1 1.9 collective-permute-start.2
  60.3 6.8 %collective-permute-done.2 = bf16[128,384]{0,1:T(8,128)(2,1)} collective-permute-done((bf16[128,384]{0,1:T(8,128)(2,1)}, bf16[128,384]{0,1:T(8,128)(2,1)}, u32[]{:S(2)}, u32[]{:S(2)}) %collective-permute-start.2) | collective-permute-done | bytes 98336 | tf_op jit(solution)/shard_map/ppermute | solution.py:458
  68.3 2.1 collective-permute-start.5
  74.4 2.9 collective-permute-done.5
  80.1 11.0 %collective-permute-done.6 = bf16[128,384]{0,1:T(8,128)(2,1)S(1)} collective-permute-done((bf16[128,384]{0,1:T(8,128)(2,1)}, bf16[128,384]{0,1:T(8,128)(2,1)S(1)}, u32[]{:S(2)}, u32[]{:S(2)}) %collective-permute-start.6) | collective-permute-done | bytes 98336 | tf_op jit(solution)/shard_map/ppermute | solution.py:456
  91.7 7.4 %collective-permute-start.12 = (bf16[128,1024]{1,0:T(8,128)(2,1)}, bf16[128,1024]{1,0:T(8,128)(2,1)S(1)}, u32[]{:S(2)}, u32[]{:S(2)}) collective-permute-start(bf16[128,1024]{1,0:T(8,128)(2,1)} %collective-permute-done.10), channel_id=1, source_target_pairs={{0,8},{8,16},{16,24},{24,28},{28,20},{20,12},{12,4},{4,0},{1,9},{9... | collective-permute-start | bytes 786440 | tf_op jit(solution)/shard_map/ppermute | solution.py:456
  99.7 5.4 %collective-permute-start.11 = (bf16[128,1024]{1,0:T(8,128)(2,1)S(1)}, bf16[128,1024]{1,0:T(8,128)(2,1)S(1)}, u32[]{:S(2)}, u32[]{:S(2)}) collective-permute-start(bf16[128,1024]{1,0:T(8,128)(2,1)S(1)} %collective-permute-done.9), channel_id=1, source_target_pairs={{8,0},{16,8},{24,16},{28,24},{20,28},{12,20},{4,12},{0,4},{9,1},{1... | collective-permute-start | bytes 786440 | tf_op jit(solution)/shard_map/ppermute | solution.py:458
  106.0 5.3 %first_norm.2 = (f32[1024,1024]{1,0:T(8,128)}, bf16[1024,1024]{1,0:T(8,128)(2,1)}) custom-call(f32[1024,1024]{1,0:T(8,128)} %embed.2.x, f32[1,1024]{1,0:T(1,128)} %get-tuple-element.195.cond, f32[1,1024]{1,0:T(1,128)} %bitcast.96), custom_call_target="tpu_custom_call" | custom-call | tf_op jit(solution)/shard_map/first_norm/pallas_call | solution.py:120
  112.9 5.3 %collective-permute-done.13 = bf16[128,1024]{1,0:T(8,128)(2,1)S(1)} collective-permute-done((bf16[128,1024]{1,0:T(8,128)(2,1)S(1)}, bf16[128,1024]{1,0:T(8,128)(2,1)S(1)}, u32[]{:S(2)}, u32[]{:S(2)}) %collective-permute-start.13) | collective-permute-done | bytes 262176 | tf_op jit(solution)/shard_map/ppermute | solution.py:456
  119.6 14.9 %attend.2 = (bf16[1024,768]{1,0:T(8,128)(2,1)}, bf16[1024,256]{1,0:T(8,128)(2,1)}, f32[1024,128]{1,0:T(8,128)}, bf16[512,1024]{1,0:T(8,128)(2,1)}, bf16[512,1024]{1,0:T(8,128)(2,1)}) custom-call(s32[9]{0:T(128)} %pad_add_fusion.meta, bf16[1024,1024]{1,0:T(8,128)(2,1)} %get-tuple-element.55.n1, bf16[1024,1024]{1,0:T(8,128)(2,1)} %copy-done.4, ...), custom_call_target="tpu_custom_call" | custom-call | tf_op jit(solution)/shard_map/attend/pallas_call | solution.py:201
  134.5 2.9 collective-permute-done.14
  137.4 1.6 add_convert_fusion.3
  139.0 1.5 collective-permute-start.15
  140.7 23.6 %collective-permute-done.15 = bf16[512,1024]{1,0:T(8,128)(2,1)S(1)} collective-permute-done((bf16[512,1024]{1,0:T(8,128)(2,1)S(1)}, bf16[512,1024]{1,0:T(8,128)(2,1)S(1)}, u32[]{:S(2)}, u32[]{:S(2)}) %collective-permute-start.15) | collective-permute-done | bytes 1048608 | tf_op jit(solution)/shard_map/ppermute | solution.py:485
  164.3 2.0 fusion.85
  171.2 10.9 %embed.3.x = f32[1024,1024]{1,0:T(8,128)} custom-call(s32[9]{0:T(128)} %pad_add_fusion.1.meta, bf16[1024,1024]{1,0:T(8,128)(2,1)} %get-tuple-element.163.x, s32[1024,1]{1,0:T(8,128)} %sub.94.place, f32[1,512]{1,0:T(1,128)} %multiply_exponential_fusion.freq), custom_call_target="tpu_custom_call" | custom-call | tf_op jit(solution)/shard_map/embed/pallas_call | solution.py:91
  182.2 5.6 %first_norm.3 = (f32[1024,1024]{1,0:T(8,128)}, bf16[1024,1024]{1,0:T(8,128)(2,1)}) custom-call(f32[1024,1024]{1,0:T(8,128)} %embed.3.x, f32[1,1024]{1,0:T(1,128)} %get-tuple-element.196.cond, f32[1,1024]{1,0:T(1,128)} %bitcast.97), custom_call_target="tpu_custom_call" | custom-call | tf_op jit(solution)/shard_map/first_norm/pallas_call | solution.py:120
  187.7 15.3 %attend.3 = (bf16[1024,768]{1,0:T(8,128)(2,1)}, bf16[1024,256]{1,0:T(8,128)(2,1)}, f32[1024,128]{1,0:T(8,128)}, bf16[512,1024]{1,0:T(8,128)(2,1)}, bf16[512,1024]{1,0:T(8,128)(2,1)}) custom-call(s32[9]{0:T(128)} %pad_add_fusion.1.meta, bf16[1024,1024]{1,0:T(8,128)(2,1)} %get-tuple-element.65.n1, bf16[1024,1024]{1,0:T(8,128)(2,1)} %copy-done.4, ...), custom_call_target="tpu_custom_call" | custom-call | tf_op jit(solution)/shard_map/attend/pallas_call | solution.py:201
  203.4 3.3 fusion.87
  206.7 9.4 %hidden_layer.4 = (bf16[2048,1024]{1,0:T(8,128)(2,1)}, bf16[2048,1024]{1,0:T(8,128)(2,1)}, bf16[512,1024]{1,0:T(8,128)(2,1)}, bf16[2,1024,256]{2,1,0:T(8,128)(2,1)}, bf16[2,1024,256]{2,1,0:T(8,128)(2,1)}) custom-call(s32[9]{0:T(128)} %pad_add_fusion.meta, bf16[512,1024]{1,0:T(8,128)(2,1)} %copy-done.15, bf16[1024,1024]{1,0:T(8,128)(2,1)} %get-tuple-element.159.cot, ...), custom_call_target="tpu_custom_call" | custom-call | tf_op jit(solution)/shard_map/hidden_layer/pallas_call | solution.py:278
  216.1 9.3 %hidden_layer.5 = (bf16[2048,1024]{1,0:T(8,128)(2,1)}, bf16[2048,1024]{1,0:T(8,128)(2,1)}, bf16[512,1024]{1,0:T(8,128)(2,1)}, bf16[2,1024,256]{2,1,0:T(8,128)(2,1)}, bf16[2,1024,256]{2,1,0:T(8,128)(2,1)}) custom-call(s32[9]{0:T(128)} %pad_add_fusion.meta, ...), custom_call_target="tpu_custom_call", output_to_operand_aliasing={{0}: (4, {}), {1}: (5, {}), {3}: (6, {}), {4}: (7, {})} | custom-call | tf_op jit(solution)/shard_map/hidden_layer/pallas_call | solution.py:278
  225.6 2.7 add_convert_fusion.2
  230.7 23.8 %collective-permute-done.20 = bf16[512,1024]{1,0:T(8,128)(2,1)} collective-permute-done((bf16[512,1024]{1,0:T(8,128)(2,1)}, bf16[512,1024]{1,0:T(8,128)(2,1)}, u32[]{:S(2)}, u32[]{:S(2)}) %collective-permute-start.20) | collective-permute-done | bytes 1048608 | tf_op jit(solution)/shard_map/ppermute | solution.py:485
  254.5 2.6 fusion.86
  257.6 18.8 %collective-permute-done.25 = bf16[512,1024]{1,0:T(8,128)(2,1)} collective-permute-done((bf16[512,1024]{1,0:T(8,128)(2,1)S(1)}, bf16[512,1024]{1,0:T(8,128)(2,1)}, u32[]{:S(2)}, u32[]{:S(2)}) %collective-permute-start.25) | collective-permute-done | bytes 1048608 | tf_op jit(solution)/shard_map/ppermute | solution.py:485
  276.4 2.2 multiply_reduce_fusion.1
  278.7 3.9 fusion.83
  282.6 5.1 fusion.27
  291.6 1.6 convert_add_fusion.7
  295.7 9.4 %hidden_layer.6 = (bf16[2048,1024]{1,0:T(8,128)(2,1)}, bf16[2048,1024]{1,0:T(8,128)(2,1)}, bf16[512,1024]{1,0:T(8,128)(2,1)}, bf16[2,1024,256]{2,1,0:T(8,128)(2,1)}, bf16[2,1024,256]{2,1,0:T(8,128)(2,1)}) custom-call(s32[9]{0:T(128)} %pad_add_fusion.1.meta, bf16[512,1024]{1,0:T(8,128)(2,1)} %get-tuple-element.200.n2, ...), custom_call_target="tpu_custom_call", output_to_operand_aliasing={{0}: (5, {}), {1}: (6, {})} | custom-call | tf_op jit(solution)/shard_map/hidden_layer/pallas_call | solution.py:278
  305.1 9.5 %hidden_layer.7 = (bf16[2048,1024]{1,0:T(8,128)(2,1)}, bf16[2048,1024]{1,0:T(8,128)(2,1)}, bf16[512,1024]{1,0:T(8,128)(2,1)}, bf16[2,1024,256]{2,1,0:T(8,128)(2,1)}, bf16[2,1024,256]{2,1,0:T(8,128)(2,1)}) custom-call(s32[9]{0:T(128)} %pad_add_fusion.1.meta, ...), custom_call_target="tpu_custom_call", output_to_operand_aliasing={{0}: (4, {}), {1}: (5, {}), {3}: (6, {}), {4}: (7, {})} | custom-call | tf_op jit(solution)/shard_map/hidden_layer/pallas_call | solution.py:278
  315.0 7.8 %fusion.34 = bf16[1024,1024]{0,1:T(8,128)(2,1)S(1)} fusion(bf16[2048,1024]{1,0:T(8,128)(2,1)} %get-tuple-element.94, bf16[512,1024]{1,0:T(8,128)(2,1)} %collective-permute-done.21.n2, bf16[512,1024]{1,0:T(8,128)(2,1)} %get-tuple-element.200.n2, bf16[512,1024]{1,0:T(8,128)(2,1)} %collective-permute-done.16.n2, bf16[512,1024]{1,0:T(8,128)(2,1)S(1)} %copy-done.16), kind=kOutput, calls=%fused_computation.85 | convolution fusion | flops 4312793088 | bytes 10485760 | tf_op jit(solution)/shard_map/ki,kj->ij/dot_general | solution.py:433
  322.9 4.9 fusion.31
  329.1 23.1 %attend_back.2 = (bf16[1024,768]{1,0:T(8,128)(2,1)}, bf16[2,1024,256]{2,1,0:T(8,128)(2,1)}, bf16[2,1024,256]{2,1,0:T(8,128)(2,1)}, f32[8,1024]{1,0:T(8,128)}) custom-call(s32[9]{0:T(128)} %pad_add_fusion.meta, bf16[512,1024]{1,0:T(8,128)(2,1)} %get-tuple-element.146.low_own, bf16[512,1024]{1,0:T(8,128)(2,1)} %collective-permute-done.26.low_other, ...), custom_call_target="tpu_custom_call" | custom-call | tf_op jit(solution)/shard_map/attend_back/pallas_call | solution.py:412
  352.6 2.2 fusion.67
  354.8 2.0 collective-permute-start.45
  358.3 1.7 add_convert_fusion
  364.1 22.0 %collective-permute-done.30 = bf16[512,1024]{1,0:T(8,128)(2,1)S(1)} collective-permute-done((bf16[512,1024]{1,0:T(8,128)(2,1)S(1)}, bf16[512,1024]{1,0:T(8,128)(2,1)S(1)}, u32[]{:S(2)}, u32[]{:S(2)}) %collective-permute-start.30) | collective-permute-done | bytes 1048608 | tf_op jit(solution)/shard_map/ppermute | solution.py:485
  387.0 2.3 fusion.84
  391.5 5.8 %collective-permute-done.28 = bf16[1,1024,256]{2,1,0:T(8,128)(2,1)S(1)} collective-permute-done((bf16[1,1024,256]{2,1,0:T(8,128)(2,1)S(1)}, bf16[1,1024,256]{2,1,0:T(8,128)(2,1)S(1)}, u32[]{:S(2)}, u32[]{:S(2)}) %collective-permute-start.28) | collective-permute-done | bytes 524320 | tf_op jit(solution)/shard_map/ppermute | solution.py:485
  397.9 10.0 %collective-permute-done.23 = bf16[1,1024,256]{2,1,0:T(8,128)(2,1)S(1)} collective-permute-done((bf16[1,1024,256]{2,1,0:T(8,128)(2,1)S(1)}, bf16[1,1024,256]{2,1,0:T(8,128)(2,1)S(1)}, u32[]{:S(2)}, u32[]{:S(2)}) %collective-permute-start.23) | collective-permute-done | bytes 524320 | tf_op jit(solution)/shard_map/ppermute | solution.py:485
  409.1 23.5 %attend_back.3 = (bf16[1024,768]{1,0:T(8,128)(2,1)}, bf16[2,1024,256]{2,1,0:T(8,128)(2,1)}, bf16[2,1024,256]{2,1,0:T(8,128)(2,1)}, f32[8,1024]{1,0:T(8,128)}) custom-call(s32[9]{0:T(128)} %pad_add_fusion.1.meta, bf16[512,1024]{1,0:T(8,128)(2,1)} %copy-done.17, bf16[512,1024]{1,0:T(8,128)(2,1)} %copy-done.25, bf16[1024,1024]{1,0:T(8,128)(2,1)} %copy-done.4, ...), custom_call_target="tpu_custom_call" | custom-call | tf_op jit(solution)/shard_map/attend_back/pallas_call | solution.py:412
  432.7 6.1 %fusion.37 = bf16[1024,768]{0,1:T(8,128)(2,1)S(1)} fusion(bf16[1024,768]{1,0:T(8,128)(2,1)} %get-tuple-element.91, bf16[1024,768]{1,0:T(8,128)(2,1)} %get-tuple-element.90, bf16[1024,1024]{1,0:T(8,128)(2,1)} %get-tuple-element.65.n1, bf16[1024,1024]{1,0:T(8,128)(2,1)S(1)} %copy-done.20), kind=kOutput, calls=%fused_computation.86 | convolution fusion | flops 3236691968 | bytes 8912896 | tf_op jit(solution)/shard_map/ki,kj->ij/dot_general | solution.py:433
  439.8 2.5 fusion.44
  442.8 1.5 add_convert_fusion.6
  444.4 2.0 collective-permute-start.46
  448.2 1.6 collective-permute-start.38
  449.8 2.9 collective-permute-done.34
  452.9 6.7 %collective-permute-done.46 = bf16[128,2048]{0,1:T(8,128)(2,1)S(1)} collective-permute-done((bf16[128,2048]{0,1:T(8,128)(2,1)S(1)}, bf16[128,2048]{0,1:T(8,128)(2,1)S(1)}, u32[]{:S(2)}, u32[]{:S(2)}) %collective-permute-start.46) | collective-permute-done | bytes 524320 | tf_op jit(solution)/shard_map/ppermute | solution.py:476
  459.8 1.7 collective-permute-start.47
  462.6 3.4 collective-permute-done.38
  465.9 2.9 collective-permute-done.35
  470.1 1.8 collective-permute-start.39
  471.8 5.3 %collective-permute-done.47 = bf16[128,2048]{0,1:T(8,128)(2,1)S(1)} collective-permute-done((bf16[128,2048]{0,1:T(8,128)(2,1)S(1)}, bf16[128,2048]{0,1:T(8,128)(2,1)S(1)}, u32[]{:S(2)}, u32[]{:S(2)}) %collective-permute-start.47) | collective-permute-done | bytes 524320 | tf_op jit(solution)/shard_map/ppermute | solution.py:476
  478.4 2.0 copy.104
  483.0 1.7 collective-permute-start.37
  488.2 2.2 collective-permute-done.37
  494.8 6.2 %collective-permute-done.49 = f32[128,128]{0,1:T(8,128)} collective-permute-done((f32[128,128]{0,1:T(8,128)}, f32[128,128]{0,1:T(8,128)}, u32[]{:S(2)}, u32[]{:S(2)}) %collective-permute-start.49) | collective-permute-done | bytes 65568 | tf_op jit(solution)/shard_map/ppermute | solution.py:485
  (290 shorter events, 77.0 us)
Async XLA Ops:
  7.2 10.9 %copy-start.34 = (bf16[1024,128]{1,0:T(8,128)(2,1)S(1)}, bf16[1024,128]{1,0:T(8,128)(2,1)}, u32[]{:S(2)}) copy-start(bf16[1024,128]{1,0:T(8,128)(2,1)} %param.27) | copy-start | bytes 786436
  7.2 199.5 %all-gather.2.cloned.1.call-start = ((), (), s32[]{:S(2)}) async-start(), calls=%async_computation | async-start | bytes 4718592 | tf_op jit(solution)/shard_map/all_gather | solution.py:547
  8.2 10.1 %copy-start.35 = (bf16[128,1024]{1,0:T(8,128)(2,1)S(1)}, bf16[128,1024]{1,0:T(8,128)(2,1)}, u32[]{:S(2)}) copy-start(bf16[128,1024]{1,0:T(8,128)(2,1)} %param.26) | copy-start | bytes 786436
  10.0 46.0 %collective-permute-start = (bf16[128,384]{0,1:T(8,128)(2,1)S(1)}, bf16[128,384]{0,1:T(8,128)(2,1)}, u32[]{:S(2)}, u32[]{:S(2)}) collective-permute-start(bf16[128,384]{0,1:T(8,128)(2,1)S(1)} %concatenate.74), channel_id=1, source_target_pairs={{8,0},{16,8},{24,16},{28,24},{20,28},{12,20},{4,12},{0,4},{9,1},{1... | collective-permute-start | bytes 294920 | tf_op jit(solution)/shard_map/ppermute | solution.py:458
  13.0 46.0 %collective-permute-start.1 = (bf16[128,384]{0,1:T(8,128)(2,1)S(1)}, bf16[128,384]{0,1:T(8,128)(2,1)}, u32[]{:S(2)}, u32[]{:S(2)}) collective-permute-start(bf16[128,384]{0,1:T(8,128)(2,1)S(1)} %concatenate.74), channel_id=1, source_target_pairs={{0,8},{8,16},{16,24},{24,28},{28,20},{20,12},{12,4},{4,0},{1,9},{9... | collective-permute-start | bytes 294920 | tf_op jit(solution)/shard_map/ppermute | solution.py:456
  16.1 54.3 %collective-permute-start.7 = (bf16[128,1024]{1,0:T(8,128)(2,1)}, bf16[128,1024]{1,0:T(8,128)(2,1)}, u32[]{:S(2)}, u32[]{:S(2)}) collective-permute-start(bf16[128,1024]{1,0:T(8,128)(2,1)} %get-tuple-element.184), channel_id=1, source_target_pairs={{8,0},{16,8},{24,16},{28,24},{20,28},{12,20},{4,12},{0,4},{9,1},{1... | collective-permute-start | bytes 786440 | tf_op jit(solution)/shard_map/ppermute | solution.py:458
  18.0 53.7 %collective-permute-start.8 = (bf16[128,1024]{1,0:T(8,128)(2,1)}, bf16[128,1024]{1,0:T(8,128)(2,1)}, u32[]{:S(2)}, u32[]{:S(2)}) collective-permute-start(bf16[128,1024]{1,0:T(8,128)(2,1)} %get-tuple-element.184), channel_id=1, source_target_pairs={{0,8},{8,16},{16,24},{24,28},{28,20},{20,12},{12,4},{4,0},{1,9},{9... | collective-permute-start | bytes 786440 | tf_op jit(solution)/shard_map/ppermute | solution.py:456
  21.0 14.1 %copy-start.36 = (s32[8]{0:T(128)S(1)}, s32[8]{0:T(128)}, u32[]{:S(2)}) copy-start(s32[8]{0:T(128)} %constant.317.clone) | copy-start | bytes 100
  57.1 10.0 %collective-permute-start.2 = (bf16[128,384]{0,1:T(8,128)(2,1)}, bf16[128,384]{0,1:T(8,128)(2,1)}, u32[]{:S(2)}, u32[]{:S(2)}) collective-permute-start(bf16[128,384]{0,1:T(8,128)(2,1)} %collective-permute-done), channel_id=1, source_target_pairs={{8,0},{16,8},{24,16},{28,24},{20,28},{12,20},{4,12},{0,4},{9,1},{1... | collective-permute-start | bytes 294920 | tf_op jit(solution)/shard_map/ppermute | solution.py:458
  60.0 8.1 %collective-permute-start.3 = (bf16[128,384]{0,1:T(8,128)(2,1)}, bf16[128,384]{0,1:T(8,128)(2,1)S(1)}, u32[]{:S(2)}, u32[]{:S(2)}) collective-permute-start(bf16[128,384]{0,1:T(8,128)(2,1)} %collective-permute-done.1), channel_id=1, source_target_pairs={{0,8},{8,16},{16,24},{24,28},{28,20},{20,12},{12,4},{4,0},{1,9},{9... | collective-permute-start | bytes 294920 | tf_op jit(solution)/shard_map/ppermute | solution.py:456
  68.1 11.8 %collective-permute-start.4 = (bf16[128,384]{0,1:T(8,128)(2,1)}, bf16[128,384]{0,1:T(8,128)(2,1)S(1)}, u32[]{:S(2)}, u32[]{:S(2)}) collective-permute-start(bf16[128,384]{0,1:T(8,128)(2,1)} %collective-permute-done.2), channel_id=1, source_target_pairs={{8,0},{16,8},{24,16},{28,24},{20,28},{12,20},{4,12},{0,4},{9,1},{1... | collective-permute-start | bytes 294920 | tf_op jit(solution)/shard_map/ppermute | solution.py:458
  68.3 9.1 %collective-permute-start.5 = (bf16[128,384]{0,1:T(8,128)(2,1)S(1)}, bf16[128,384]{0,1:T(8,128)(2,1)}, u32[]{:S(2)}, u32[]{:S(2)}) collective-permute-start(bf16[128,384]{0,1:T(8,128)(2,1)S(1)} %collective-permute-done.3), channel_id=1, source_target_pairs={{0,8},{8,16},{16,24},{24,28},{28,20},{20,12},{12,4},{4,0},{1,9},{9... | collective-permute-start | bytes 294920 | tf_op jit(solution)/shard_map/ppermute | solution.py:456
  70.4 29.3 %collective-permute-start.9 = (bf16[128,1024]{1,0:T(8,128)(2,1)}, bf16[128,1024]{1,0:T(8,128)(2,1)S(1)}, u32[]{:S(2)}, u32[]{:S(2)}) collective-permute-start(bf16[128,1024]{1,0:T(8,128)(2,1)} %collective-permute-done.7), channel_id=1, source_target_pairs={{8,0},{16,8},{24,16},{28,24},{20,28},{12,20},{4,12},{0,4},{9,1},{1... | collective-permute-start | bytes 786440 | tf_op jit(solution)/shard_map/ppermute | solution.py:458
  71.6 20.0 %collective-permute-start.10 = (bf16[128,1024]{1,0:T(8,128)(2,1)}, bf16[128,1024]{1,0:T(8,128)(2,1)}, u32[]{:S(2)}, u32[]{:S(2)}) collective-permute-start(bf16[128,1024]{1,0:T(8,128)(2,1)} %collective-permute-done.8), channel_id=1, source_target_pairs={{0,8},{8,16},{16,24},{24,28},{28,20},{20,12},{12,4},{4,0},{1,9},{9... | collective-permute-start | bytes 786440 | tf_op jit(solution)/shard_map/ppermute | solution.py:456
  78.3 12.7 %collective-permute-start.6 = (bf16[128,384]{0,1:T(8,128)(2,1)}, bf16[128,384]{0,1:T(8,128)(2,1)S(1)}, u32[]{:S(2)}, u32[]{:S(2)}) collective-permute-start(bf16[128,384]{0,1:T(8,128)(2,1)} %collective-permute-done.5), channel_id=1, source_target_pairs={{0,8},{8,16},{16,24},{24,28},{28,20},{20,12},{12,4},{4,0},{1,9},{9... | collective-permute-start | bytes 294920 | tf_op jit(solution)/shard_map/ppermute | solution.py:456
  80.0 11.3 %copy-start.38 = (f32[2,256]{1,0:T(2,128)S(1)}, f32[2,256]{1,0:T(2,128)}, u32[]{:S(2)}) copy-start(f32[2,256]{1,0:T(2,128)} %pad_maximum_fusion.5) | copy-start | bytes 6148
  91.2 20.1 %copy-start.11 = (bf16[1024,384]{1,0:T(8,128)(2,1)}, bf16[1024,384]{1,0:T(8,128)(2,1)S(1)}, u32[]{:S(2)}) copy-start(bf16[1024,384]{1,0:T(8,128)(2,1)S(1)} %constant_dynamic-update-slice_fusion.10) | copy-start | bytes 2359300
  91.7 19.6 %collective-permute-start.12 = (bf16[128,1024]{1,0:T(8,128)(2,1)}, bf16[128,1024]{1,0:T(8,128)(2,1)S(1)}, u32[]{:S(2)}, u32[]{:S(2)}) collective-permute-start(bf16[128,1024]{1,0:T(8,128)(2,1)} %collective-permute-done.10), channel_id=1, source_target_pairs={{0,8},{8,16},{16,24},{24,28},{28,20},{20,12},{12,4},{4,0},{1,9},{9... | collective-permute-start | bytes 786440 | tf_op jit(solution)/shard_map/ppermute | solution.py:456
  99.7 13.2 %collective-permute-start.11 = (bf16[128,1024]{1,0:T(8,128)(2,1)S(1)}, bf16[128,1024]{1,0:T(8,128)(2,1)S(1)}, u32[]{:S(2)}, u32[]{:S(2)}) collective-permute-start(bf16[128,1024]{1,0:T(8,128)(2,1)S(1)} %collective-permute-done.9), channel_id=1, source_target_pairs={{8,0},{16,8},{24,16},{28,24},{20,28},{12,20},{4,12},{0,4},{9,1},{1... | collective-permute-start | bytes 786440 | tf_op jit(solution)/shard_map/ppermute | solution.py:458
  111.3 6.9 %collective-permute-start.13 = (bf16[128,1024]{1,0:T(8,128)(2,1)S(1)}, bf16[128,1024]{1,0:T(8,128)(2,1)S(1)}, u32[]{:S(2)}, u32[]{:S(2)}) collective-permute-start(bf16[128,1024]{1,0:T(8,128)(2,1)S(1)} %collective-permute-done.12), channel_id=1, source_target_pairs={{0,8},{8,16},{16,24},{24,28},{28,20},{20,12},{12,4},{4,0},{1,9},{9... | collective-permute-start | bytes 786440 | tf_op jit(solution)/shard_map/ppermute | solution.py:456
  134.5 2.9 collective-permute-start.14
  139.0 25.3 %collective-permute-start.15 = (bf16[512,1024]{1,0:T(8,128)(2,1)S(1)}, bf16[512,1024]{1,0:T(8,128)(2,1)S(1)}, u32[]{:S(2)}, u32[]{:S(2)}) collective-permute-start(bf16[512,1024]{1,0:T(8,128)(2,1)S(1)} %add_convert_fusion.3), channel_id=1, source_target_pairs={{0,2},{1,3},{2,0},{3,1},{4,6},{5,7},{6,4},{7,5},{8,10},{9,11},{10,... | collective-permute-start | bytes 3145736 | tf_op jit(solution)/shard_map/ppermute | solution.py:485
  167.6 14.6 %copy-start.15 = (bf16[512,1024]{1,0:T(8,128)(2,1)}, bf16[512,1024]{1,0:T(8,128)(2,1)S(1)}, u32[]{:S(2)}) copy-start(bf16[512,1024]{1,0:T(8,128)(2,1)S(1)} %multiply_convert_fusion.1.n2) | copy-start | bytes 3145732
  167.6 48.5 %collective-permute-start.16 = (bf16[512,1024]{1,0:T(8,128)(2,1)S(1)}, bf16[512,1024]{1,0:T(8,128)(2,1)}, u32[]{:S(2)}, u32[]{:S(2)}) collective-permute-start(bf16[512,1024]{1,0:T(8,128)(2,1)S(1)} %multiply_convert_fusion.1.n2), channel_id=1, source_target_pairs={{0,1},{1,0},{2,3},{3,2},{4,5},{5,4},{6,7},{7,6},{8,9},{9,8},{10,11... | collective-permute-start | bytes 3145736 | tf_op jit(solution)/shard_map/ppermute | solution.py:485
  187.7 15.7 %copy-start.12 = (bf16[2,1024,1024]{2,1,0:T(8,128)(2,1)S(1)}, bf16[2,1024,1024]{2,1,0:T(8,128)(2,1)}, u32[]{:S(2)}) copy-start(bf16[2,1024,1024]{2,1,0:T(8,128)(2,1)} %param.31) | copy-start | bytes 12582916
  203.0 22.5 %collective-permute-start.19 = (bf16[512,1024]{1,0:T(8,128)(2,1)}, bf16[512,1024]{1,0:T(8,128)(2,1)}, u32[]{:S(2)}, u32[]{:S(2)}) collective-permute-start(bf16[512,1024]{1,0:T(8,128)(2,1)} %get-tuple-element.67), channel_id=1, source_target_pairs={{0,1},{1,0},{2,3},{3,2},{4,5},{5,4},{6,7},{7,6},{8,9},{9,8},{10,11... | collective-permute-start | bytes 3145736 | tf_op jit(solution)/shard_map/ppermute | solution.py:485
  225.4 4.3 collective-permute-start.24
  228.2 26.3 %collective-permute-start.20 = (bf16[512,1024]{1,0:T(8,128)(2,1)}, bf16[512,1024]{1,0:T(8,128)(2,1)}, u32[]{:S(2)}, u32[]{:S(2)}) collective-permute-start(bf16[512,1024]{1,0:T(8,128)(2,1)} %add_convert_fusion.2), channel_id=1, source_target_pairs={{0,2},{1,3},{2,0},{3,1},{4,6},{5,7},{6,4},{7,5},{8,10},{9,11},{10,... | collective-permute-start | bytes 3145736 | tf_op jit(solution)/shard_map/ppermute | solution.py:485
  230.1 46.3 %collective-permute-start.25 = (bf16[512,1024]{1,0:T(8,128)(2,1)S(1)}, bf16[512,1024]{1,0:T(8,128)(2,1)}, u32[]{:S(2)}, u32[]{:S(2)}) collective-permute-start(bf16[512,1024]{1,0:T(8,128)(2,1)S(1)} %add_convert_fusion.1), channel_id=1, source_target_pairs={{0,2},{1,3},{2,0},{3,1},{4,6},{5,7},{6,4},{7,5},{8,10},{9,11},{10,... | collective-permute-start | bytes 3145736 | tf_op jit(solution)/shard_map/ppermute | solution.py:485
  257.2 21.5 %copy-start = (f32[512,1024]{1,0:T(8,128)}, f32[512,1024]{1,0:T(8,128)S(1)}, u32[]{:S(2)}) copy-start(f32[512,1024]{1,0:T(8,128)S(1)} %get-tuple-element.153.refs_0_) | copy-start | bytes 6291460
  257.2 19.2 %copy-start.3 = (f32[512,1024]{1,0:T(8,128)S(1)}, f32[512,1024]{1,0:T(8,128)}, u32[]{:S(2)}) copy-start(f32[512,1024]{1,0:T(8,128)} %copy-done.2) | copy-start | bytes 6291460
  257.6 32.7 %collective-permute-start.17 = (bf16[2,1024,256]{2,1,0:T(8,128)(2,1)}, bf16[2,1024,256]{2,1,0:T(8,128)(2,1)}, u32[]{:S(2)}, u32[]{:S(2)}) collective-permute-start(bf16[2,1024,256]{2,1,0:T(8,128)(2,1)} %get-tuple-element.63), channel_id=1, source_target_pairs={{0,1},{1,0},{2,3},{3,2},{4,5},{5,4},{6,7},{7,6},{8,9},{9,8},{10,11... | collective-permute-start | bytes 3145736 | tf_op jit(solution)/shard_map/ppermute | solution.py:485
  282.6 22.5 %collective-permute-start.21 = (bf16[512,1024]{1,0:T(8,128)(2,1)}, bf16[512,1024]{1,0:T(8,128)(2,1)}, u32[]{:S(2)}, u32[]{:S(2)}) collective-permute-start(bf16[512,1024]{1,0:T(8,128)(2,1)} %get-tuple-element.200.n2), channel_id=1, source_target_pairs={{0,1},{1,0},{2,3},{3,2},{4,5},{5,4},{6,7},{7,6},{8,9},{9,8},{10,11... | collective-permute-start | bytes 3145736 | tf_op jit(solution)/shard_map/ppermute | solution.py:485
  294.0 58.5 %collective-permute-start.18 = (bf16[1,1024,256]{2,1,0:T(8,128)(2,1)}, bf16[1,1024,256]{2,1,0:T(8,128)(2,1)S(1)}, u32[]{:S(2)}, u32[]{:S(2)}) collective-permute-start(bf16[1,1024,256]{2,1,0:T(8,128)(2,1)} %dynamic-slice_convert_fusion.3), channel_id=1, source_target_pairs={{0,2},{1,3},{2,0},{3,1},{4,6},{5,7},{6,4},{7,5},{8,10},{9,11},{10,... | collective-permute-start | bytes 1572872 | tf_op jit(solution)/shard_map/ppermute | solution.py:485
  295.5 33.6 %collective-permute-start.26 = (bf16[512,1024]{1,0:T(8,128)(2,1)S(1)}, bf16[512,1024]{1,0:T(8,128)(2,1)}, u32[]{:S(2)}, u32[]{:S(2)}) collective-permute-start(bf16[512,1024]{1,0:T(8,128)(2,1)S(1)} %copy-done.13), channel_id=1, source_target_pairs={{0,1},{1,0},{2,3},{3,2},{4,5},{5,4},{6,7},{7,6},{8,9},{9,8},{10,11... | collective-permute-start | bytes 3145736 | tf_op jit(solution)/shard_map/ppermute | solution.py:485
  314.6 43.7 %collective-permute-start.29 = (bf16[512,1024]{1,0:T(8,128)(2,1)}, bf16[512,1024]{1,0:T(8,128)(2,1)}, u32[]{:S(2)}, u32[]{:S(2)}) collective-permute-start(bf16[512,1024]{1,0:T(8,128)(2,1)} %get-tuple-element.84), channel_id=1, source_target_pairs={{0,1},{1,0},{2,3},{3,2},{4,5},{5,4},{6,7},{7,6},{8,9},{9,8},{10,11... | collective-permute-start | bytes 3145736 | tf_op jit(solution)/shard_map/ppermute | solution.py:485
  329.0 27.9 %collective-permute-start.41 = (bf16[128,2048]{0,1:T(8,128)(2,1)}, bf16[128,2048]{0,1:T(8,128)(2,1)}, u32[]{:S(2)}, u32[]{:S(2)}) collective-permute-start(bf16[128,2048]{0,1:T(8,128)(2,1)} %get-tuple-element.156), channel_id=1, source_target_pairs={{0,8},{8,16},{16,24},{24,28},{28,20},{20,12},{12,4},{4,0},{1,9},{9... | collective-permute-start | bytes 1572872 | tf_op jit(solution)/shard_map/ppermute | solution.py:476
  352.3 8.4 %collective-permute-start.27 = (bf16[2,1024,256]{2,1,0:T(8,128)(2,1)}, bf16[2,1024,256]{2,1,0:T(8,128)(2,1)S(1)}, u32[]{:S(2)}, u32[]{:S(2)}) collective-permute-start(bf16[2,1024,256]{2,1,0:T(8,128)(2,1)} %get-tuple-element.82), channel_id=1, source_target_pairs={{0,1},{1,0},{2,3},{3,2},{4,5},{5,4},{6,7},{7,6},{8,9},{9,8},{10,11... | collective-permute-start | bytes 3145736 | tf_op jit(solution)/shard_map/ppermute | solution.py:485
  354.8 88.0 %collective-permute-start.45 = (bf16[128,2048]{0,1:T(8,128)(2,1)}, bf16[128,2048]{0,1:T(8,128)(2,1)}, u32[]{:S(2)}, u32[]{:S(2)}) collective-permute-start(bf16[128,2048]{0,1:T(8,128)(2,1)} %get-tuple-element.157), channel_id=1, source_target_pairs={{8,0},{16,8},{24,16},{28,24},{20,28},{12,20},{4,12},{0,4},{9,1},{1... | collective-permute-start | bytes 1572872 | tf_op jit(solution)/shard_map/ppermute | solution.py:476
  356.8 5.8 %collective-permute-start.22 = (bf16[2,1024,256]{2,1,0:T(8,128)(2,1)S(1)}, bf16[2,1024,256]{2,1,0:T(8,128)(2,1)S(1)}, u32[]{:S(2)}, u32[]{:S(2)}) collective-permute-start(bf16[2,1024,256]{2,1,0:T(8,128)(2,1)S(1)} %copy-done.29), channel_id=1, source_target_pairs={{0,1},{1,0},{2,3},{3,2},{4,5},{5,4},{6,7},{7,6},{8,9},{9,8},{10,11... | collective-permute-start | bytes 3145736 | tf_op jit(solution)/shard_map/ppermute | solution.py:485
  358.2 31.1 %collective-permute-start.42 = (bf16[128,2048]{0,1:T(8,128)(2,1)S(1)}, bf16[128,2048]{0,1:T(8,128)(2,1)S(1)}, u32[]{:S(2)}, u32[]{:S(2)}) collective-permute-start(bf16[128,2048]{0,1:T(8,128)(2,1)S(1)} %add_convert_fusion.8), channel_id=1, source_target_pairs={{0,8},{8,16},{16,24},{24,28},{28,20},{20,12},{12,4},{4,0},{1,9},{9... | collective-permute-start | bytes 1572872 | tf_op jit(solution)/shard_map/ppermute | solution.py:476
  360.0 26.1 %collective-permute-start.30 = (bf16[512,1024]{1,0:T(8,128)(2,1)S(1)}, bf16[512,1024]{1,0:T(8,128)(2,1)S(1)}, u32[]{:S(2)}, u32[]{:S(2)}) collective-permute-start(bf16[512,1024]{1,0:T(8,128)(2,1)S(1)} %add_convert_fusion), channel_id=1, source_target_pairs={{0,2},{1,3},{2,0},{3,1},{4,6},{5,7},{6,4},{7,5},{8,10},{9,11},{10,... | collective-permute-start | bytes 3145736 | tf_op jit(solution)/shard_map/ppermute | solution.py:485
  361.1 36.2 %collective-permute-start.28 = (bf16[1,1024,256]{2,1,0:T(8,128)(2,1)S(1)}, bf16[1,1024,256]{2,1,0:T(8,128)(2,1)S(1)}, u32[]{:S(2)}, u32[]{:S(2)}) collective-permute-start(bf16[1,1024,256]{2,1,0:T(8,128)(2,1)S(1)} %dynamic-slice_convert_fusion.1), channel_id=1, source_target_pairs={{0,2},{1,3},{2,0},{3,1},{4,6},{5,7},{6,4},{7,5},{8,10},{9,11},{10,... | collective-permute-start | bytes 1572872 | tf_op jit(solution)/shard_map/ppermute | solution.py:485
  362.7 23.4 %copy-start.1 = (f32[512,1024]{1,0:T(8,128)S(1)}, f32[512,1024]{1,0:T(8,128)}, u32[]{:S(2)}) copy-start(f32[512,1024]{1,0:T(8,128)} %copy-done) | copy-start | bytes 6291460
  363.0 24.0 %copy-start.10 = (bf16[1,1024,1024]{2,1,0:T(8,128)(2,1)S(1)}, bf16[1,1024,1024]{2,1,0:T(8,128)(2,1)}, u32[]{:S(2)}) copy-start(bf16[1,1024,1024]{2,1,0:T(8,128)(2,1)} %get-tuple-element.161) | copy-start | bytes 6291460
  363.0 44.9 %collective-permute-start.23 = (bf16[1,1024,256]{2,1,0:T(8,128)(2,1)S(1)}, bf16[1,1024,256]{2,1,0:T(8,128)(2,1)S(1)}, u32[]{:S(2)}, u32[]{:S(2)}) collective-permute-start(bf16[1,1024,256]{2,1,0:T(8,128)(2,1)S(1)} %dynamic-slice_convert_fusion.2), channel_id=1, source_target_pairs={{0,2},{1,3},{2,0},{3,1},{4,6},{5,7},{6,4},{7,5},{8,10},{9,11},{10,... | collective-permute-start | bytes 1572872 | tf_op jit(solution)/shard_map/ppermute | solution.py:485
  389.3 18.8 %collective-permute-start.31 = (bf16[512,1024]{1,0:T(8,128)(2,1)S(1)}, bf16[512,1024]{1,0:T(8,128)(2,1)S(1)}, u32[]{:S(2)}, u32[]{:S(2)}) collective-permute-start(bf16[512,1024]{1,0:T(8,128)(2,1)S(1)} %get-tuple-element.148.low_own), channel_id=1, source_target_pairs={{0,1},{1,0},{2,3},{3,2},{4,5},{5,4},{6,7},{7,6},{8,9},{9,8},{10,11... | collective-permute-start | bytes 3145736 | tf_op jit(solution)/shard_map/ppermute | solution.py:485
  390.4 52.4 %collective-permute-start.43 = (bf16[128,2048]{0,1:T(8,128)(2,1)}, bf16[128,2048]{0,1:T(8,128)(2,1)}, u32[]{:S(2)}, u32[]{:S(2)}) collective-permute-start(bf16[128,2048]{0,1:T(8,128)(2,1)} %add_convert_fusion.7), channel_id=1, source_target_pairs={{0,8},{8,16},{16,24},{24,28},{28,20},{20,12},{12,4},{4,0},{1,9},{9... | collective-permute-start | bytes 1572872 | tf_op jit(solution)/shard_map/ppermute | solution.py:476
  409.1 23.5 %copy-start.20 = (bf16[1024,1024]{1,0:T(8,128)(2,1)S(1)}, bf16[1024,1024]{1,0:T(8,128)(2,1)}, u32[]{:S(2)}) copy-start(bf16[1024,1024]{1,0:T(8,128)(2,1)} %get-tuple-element.55.n1) | copy-start | bytes 6291460
  442.7 10.0 %collective-permute-start.34 = (bf16[128,1152]{0,1:T(8,128)(2,1)S(1)}, bf16[128,1152]{0,1:T(8,128)(2,1)S(1)}, u32[]{:S(2)}, u32[]{:S(2)}) collective-permute-start(bf16[128,1152]{0,1:T(8,128)(2,1)S(1)} %get-tuple-element.168), channel_id=1, source_target_pairs={{0,8},{8,16},{16,24},{24,28},{28,20},{20,12},{12,4},{4,0},{1,9},{9... | collective-permute-start | bytes 884744 | tf_op jit(solution)/shard_map/ppermute | solution.py:476
  444.4 15.3 %collective-permute-start.46 = (bf16[128,2048]{0,1:T(8,128)(2,1)S(1)}, bf16[128,2048]{0,1:T(8,128)(2,1)S(1)}, u32[]{:S(2)}, u32[]{:S(2)}) collective-permute-start(bf16[128,2048]{0,1:T(8,128)(2,1)S(1)} %get-tuple-element.155), channel_id=1, source_target_pairs={{8,0},{16,8},{24,16},{28,24},{20,28},{12,20},{4,12},{0,4},{9,1},{1... | collective-permute-start | bytes 1572872 | tf_op jit(solution)/shard_map/ppermute | solution.py:476
  447.8 24.1 %collective-permute-start.44 = (bf16[128,2048]{0,1:T(8,128)(2,1)S(1)}, bf16[128,2048]{0,1:T(8,128)(2,1)S(1)}, u32[]{:S(2)}, u32[]{:S(2)}) collective-permute-start(bf16[128,2048]{0,1:T(8,128)(2,1)S(1)} %get-tuple-element.154), channel_id=1, source_target_pairs={{0,8},{8,16},{16,24},{24,28},{28,20},{20,12},{12,4},{4,0},{1,9},{9... | collective-permute-start | bytes 1572872 | tf_op jit(solution)/shard_map/ppermute | solution.py:476
  448.2 17.7 %collective-permute-start.38 = (bf16[128,1152]{0,1:T(8,128)(2,1)S(1)}, bf16[128,1152]{0,1:T(8,128)(2,1)S(1)}, u32[]{:S(2)}, u32[]{:S(2)}) collective-permute-start(bf16[128,1152]{0,1:T(8,128)(2,1)S(1)} %get-tuple-element.169), channel_id=1, source_target_pairs={{8,0},{16,8},{24,16},{28,24},{20,28},{12,20},{4,12},{0,4},{9,1},{1... | collective-permute-start | bytes 884744 | tf_op jit(solution)/shard_map/ppermute | solution.py:476
  452.8 16.0 %collective-permute-start.35 = (bf16[128,1152]{0,1:T(8,128)(2,1)S(1)}, bf16[128,1152]{0,1:T(8,128)(2,1)S(1)}, u32[]{:S(2)}, u32[]{:S(2)}) collective-permute-start(bf16[128,1152]{0,1:T(8,128)(2,1)S(1)} %add_convert_fusion.15), channel_id=1, source_target_pairs={{0,8},{8,16},{16,24},{24,28},{28,20},{20,12},{12,4},{4,0},{1,9},{9... | collective-permute-start | bytes 884744 | tf_op jit(solution)/shard_map/ppermute | solution.py:476
  459.8 17.4 %collective-permute-start.47 = (bf16[128,2048]{0,1:T(8,128)(2,1)S(1)}, bf16[128,2048]{0,1:T(8,128)(2,1)S(1)}, u32[]{:S(2)}, u32[]{:S(2)}) collective-permute-start(bf16[128,2048]{0,1:T(8,128)(2,1)S(1)} %add_convert_fusion.4), channel_id=1, source_target_pairs={{8,0},{16,8},{24,16},{28,24},{20,28},{12,20},{4,12},{0,4},{9,1},{1... | collective-permute-start | bytes 1572872 | tf_op jit(solution)/shard_map/ppermute | solution.py:476
  462.6 22.5 %collective-permute-start.32 = (bf16[2,1024,256]{2,1,0:T(8,128)(2,1)}, bf16[2,1024,256]{2,1,0:T(8,128)(2,1)}, u32[]{:S(2)}, u32[]{:S(2)}) collective-permute-start(bf16[2,1024,256]{2,1,0:T(8,128)(2,1)} %get-tuple-element.89), channel_id=1, source_target_pairs={{0,1},{1,0},{2,3},{3,2},{4,5},{5,4},{6,7},{7,6},{8,9},{9,8},{10,11... | collective-permute-start | bytes 3145736 | tf_op jit(solution)/shard_map/ppermute | solution.py:485
  469.8 10.6 %collective-permute-start.36 = (bf16[128,1152]{0,1:T(8,128)(2,1)}, bf16[128,1152]{0,1:T(8,128)(2,1)}, u32[]{:S(2)}, u32[]{:S(2)}) collective-permute-start(bf16[128,1152]{0,1:T(8,128)(2,1)} %get-tuple-element.166), channel_id=1, source_target_pairs={{0,8},{8,16},{16,24},{24,28},{28,20},{20,12},{12,4},{4,0},{1,9},{9... | collective-permute-start | bytes 884744 | tf_op jit(solution)/shard_map/ppermute | solution.py:476
  470.1 11.7 %collective-permute-start.39 = (bf16[128,1152]{0,1:T(8,128)(2,1)}, bf16[128,1152]{0,1:T(8,128)(2,1)}, u32[]{:S(2)}, u32[]{:S(2)}) collective-permute-start(bf16[128,1152]{0,1:T(8,128)(2,1)} %get-tuple-element.167), channel_id=1, source_target_pairs={{8,0},{16,8},{24,16},{28,24},{20,28},{12,20},{4,12},{0,4},{9,1},{1... | collective-permute-start | bytes 884744 | tf_op jit(solution)/shard_map/ppermute | solution.py:476
  483.0 7.4 %collective-permute-start.37 = (bf16[128,1152]{0,1:T(8,128)(2,1)S(1)}, bf16[128,1152]{0,1:T(8,128)(2,1)S(1)}, u32[]{:S(2)}, u32[]{:S(2)}) collective-permute-start(bf16[128,1152]{0,1:T(8,128)(2,1)S(1)} %get-tuple-element.164), channel_id=1, source_target_pairs={{0,8},{8,16},{16,24},{24,28},{28,20},{20,12},{12,4},{4,0},{1,9},{9... | collective-permute-start | bytes 884744 | tf_op jit(solution)/shard_map/ppermute | solution.py:476
  484.7 6.7 %collective-permute-start.40 = (bf16[128,1152]{0,1:T(8,128)(2,1)S(1)}, bf16[128,1152]{0,1:T(8,128)(2,1)S(1)}, u32[]{:S(2)}, u32[]{:S(2)}) collective-permute-start(bf16[128,1152]{0,1:T(8,128)(2,1)S(1)} %get-tuple-element.165), channel_id=1, source_target_pairs={{8,0},{16,8},{24,16},{28,24},{20,28},{12,20},{4,12},{0,4},{9,1},{1... | collective-permute-start | bytes 884744 | tf_op jit(solution)/shard_map/ppermute | solution.py:476
  487.6 15.9 %collective-permute-start.33 = (bf16[1,1024,256]{2,1,0:T(8,128)(2,1)}, bf16[1,1024,256]{2,1,0:T(8,128)(2,1)}, u32[]{:S(2)}, u32[]{:S(2)}) collective-permute-start(bf16[1,1024,256]{2,1,0:T(8,128)(2,1)} %dynamic-slice_convert_fusion), channel_id=1, source_target_pairs={{0,2},{1,3},{2,0},{3,1},{4,6},{5,7},{6,4},{7,5},{8,10},{9,11},{10,... | collective-permute-start | bytes 1572872 | tf_op jit(solution)/shard_map/ppermute | solution.py:485
  491.6 11.9 %copy-start.9 = (f32[2,1024,256]{2,1,0:T(8,128)S(1)}, f32[2,1024,256]{2,1,0:T(8,128)}, u32[]{:S(2)}) copy-start(f32[2,1024,256]{2,1,0:T(8,128)} %copy-done.8) | copy-start | bytes 6291460
  491.6 1.3 collective-permute-start.48
  493.6 7.5 %collective-permute-start.49 = (f32[128,128]{0,1:T(8,128)}, f32[128,128]{0,1:T(8,128)}, u32[]{:S(2)}, u32[]{:S(2)}) collective-permute-start(f32[128,128]{0,1:T(8,128)} %slice_add_fusion.2), channel_id=1, source_target_pairs={{0,2},{1,3},{2,0},{3,1},{4,6},{5,7},{6,4},{7,5},{8,10},{9,11},{10,... | collective-permute-start | bytes 196616 | tf_op jit(solution)/shard_map/ppermute | solution.py:485
  (31 other events, 157.0 us)
Sparse Core Ops, SparseCore 0:
  19.3 88.8 all-gather.1
